TPU v7x, 32 devices: a whole 2x2x4 slice. The times are simulated.
32 devices in a mesh: ctx: 16 (over z, x, core), tp: 2 (over y).
Axes of the slice: x: 2, y: 2, z: 4, core: 2. Of those that a mesh axis runs over, the one named last changes fastest.
Arguments:
- query_raw: bfloat16 [6144, 32, 128], P('ctx', 'tp'), may hold values from -12 to 12
- key_raw: bfloat16 [6144, 16, 128], P('ctx', 'tp'), may hold values from -12 to 12
- values: bfloat16 [6144, 16, 128], P('ctx', 'tp'), may hold values from -6 to 6
- query_gain: float32 [128], replicated, may hold values from 0.1 to 6
- key_gain: float32 [128], replicated, may hold values from 0.1 to 6
- documents: int32 [6144], replicated, may hold values from 0 to 3, never falling along the last dimension, each value on 1 to 3072 neighbouring positions
- upstream: bfloat16 [6144, 32, 128], P('ctx', 'tp'), may hold values from -6 to 6
Outputs:
- query_grad: bfloat16 [6144, 32, 128], P('ctx', 'tp')
- key_grad: bfloat16 [6144, 16, 128], P('ctx', 'tp')
- value_grad: bfloat16 [6144, 16, 128], P('ctx', 'tp')
- query_gain_grad: float32 [128], replicated
- key_gain_grad: float32 [128], replicated
Inputs may be any that keep to these rules, and one draw needn't show every extreme that they name: `documents`: document ids never fall along the tokens; every id from 0 to 3 occurs, each on 1 to 3072 tokens, and one document has exactly 3072 tokens.
All inputs are finite; a program needn't handle non-finite values.
Results may differ from a plain program's by a relative error of at most 0.035.
Values may be sent and summed in bfloat16 or wider, within the bound.
A program may use at most 192 MiB of HBM per device.

v0:
```python
from functools import partial
import math

import jax
import jax.numpy as jnp
from jax import lax
from jax.sharding import PartitionSpec as P

QUERY_SCALAR = 168


rope_base = 1000000.0
norm_eps = 1e-06


def from_behind(value, axis, steps):
    count = lax.axis_size(axis)
    first, last = (max(0, -steps), min(count, count - steps))
    return lax.ppermute(value, axis, [(source, source + steps) for source in range(first, last)])


def rotate(inputs, gain_vec, positions):
    meansq = jnp.mean(inputs * inputs, axis=-1, keepdims=True)
    normed = inputs * lax.rsqrt(meansq + norm_eps) * gain_vec
    half_dim = inputs.shape[-1] // 2
    inverse_freq = rope_base ** (-2.0 * jnp.arange(half_dim, dtype=jnp.float32) / inputs.shape[-1])
    angles = positions.astype(jnp.float32)[:, None] * inverse_freq[None, :]
    cosine = jnp.cos(angles)[:, None, :]
    sine_part = jnp.sin(angles)[:, None, :]
    leading = normed[..., :half_dim]
    trailing = normed[..., half_dim:]
    return jnp.concatenate(
        [leading * cosine - trailing * sine_part, trailing * cosine + leading * sine_part], axis=-1
    )


def score_block(query_half_precision, key_half_precision, visible, factor):
    products = jnp.einsum(
        "igrd,jgd->grij",
        query_half_precision,
        key_half_precision,
        preferred_element_type=jnp.float32,
    )
    return jnp.where(visible[None, None], factor * products, -1e30)


def max_update(query_half_precision, key_half_precision, visible, factor, status):
    row_peak, row_total = status
    scores = score_block(query_half_precision, key_half_precision, visible, factor)
    new_peak = jnp.maximum(row_peak, jnp.max(scores, axis=-1))
    row_total = row_total * jnp.exp(row_peak - new_peak) + jnp.sum(
        jnp.exp(scores - new_peak[..., None]), axis=-1
    )
    return (new_peak, row_total)


def unchanged(status):
    return status


def block_attend(
    query_half_precision,
    key_half_precision,
    value_bf,
    visible,
    incoming_gradient_groups,
    log_norm,
    factor,
):
    scores = score_block(query_half_precision, key_half_precision, visible, factor)
    attend = jnp.where(visible[None, None], jnp.exp(scores - log_norm[..., None]), 0.0)
    attend_bf = attend.astype(jnp.bfloat16)
    attend_grad = jnp.einsum(
        "igrd,jgd->grij", incoming_gradient_groups, value_bf, preferred_element_type=jnp.float32
    )
    return (attend, attend_bf, attend_grad)


def delta_update(
    query_half_precision,
    key_half_precision,
    value_bf,
    visible,
    incoming_gradient_groups,
    log_norm,
    factor,
    row_delta,
):
    attend, attend_bf, attend_grad = block_attend(
        query_half_precision,
        key_half_precision,
        value_bf,
        visible,
        incoming_gradient_groups,
        log_norm,
        factor,
    )
    return row_delta + jnp.sum(attend_bf.astype(jnp.float32) * attend_grad, axis=-1)


def grad_update(
    query_half_precision,
    key_half_precision,
    value_bf,
    visible,
    incoming_gradient_groups,
    log_norm,
    row_delta,
    factor,
    query_acc,
):
    attend, attend_bf, attend_grad = block_attend(
        query_half_precision,
        key_half_precision,
        value_bf,
        visible,
        incoming_gradient_groups,
        log_norm,
        factor,
    )
    score_grad = (attend * (attend_grad - row_delta[..., None])).astype(jnp.bfloat16)
    query_acc = query_acc + factor * jnp.einsum(
        "grij,jgd->igrd", score_grad, key_half_precision, preferred_element_type=jnp.float32
    )
    key_part = factor * jnp.einsum(
        "grij,igrd->jgd", score_grad, query_half_precision, preferred_element_type=jnp.float32
    )
    value_part = jnp.einsum(
        "grij,igrd->jgd", attend_bf, incoming_gradient_groups, preferred_element_type=jnp.float32
    )
    return (query_acc, key_part, value_part)


def skip_grads(key_half_precision, query_acc):
    empty_part = jnp.zeros(key_half_precision.shape, jnp.float32)
    return (query_acc, empty_part, empty_part)


def on_device(query_raw, key_raw, values, query_gain, key_gain, documents, upstream):
    block_rows = query_raw.shape[0]
    query_heads = query_raw.shape[1]
    groups = key_raw.shape[1]
    head_size = query_raw.shape[2]
    head_grouping = query_heads // groups
    factor = QUERY_SCALAR ** (-0.5)
    reach = min(8, lax.axis_size("ctx") // 2)
    first_row = lax.axis_index("ctx") * block_rows
    positions = first_row + jnp.arange(block_rows, dtype=jnp.int32)
    query_in = query_raw.astype(jnp.float32)
    key_in = key_raw.astype(jnp.float32)
    query_half_precision = (
        rotate(query_in, query_gain, positions)
        .astype(jnp.bfloat16)
        .reshape(block_rows, groups, head_grouping, head_size)
    )
    key_half_precision = rotate(key_in, key_gain, positions).astype(jnp.bfloat16)
    incoming_gradient_groups = upstream.reshape(block_rows, groups, head_grouping, head_size)
    query_docs = lax.dynamic_slice_in_dim(documents, first_row, block_rows)
    blocks = [(key_half_precision, values)]
    for offset in range(1, reach + 1):
        blocks.append(from_behind((key_half_precision, values), "ctx", offset))
    layouts = []
    for offset in range(reach + 1):
        key_start = first_row - offset * block_rows
        key_docs = lax.dynamic_slice_in_dim(documents, jnp.maximum(key_start, 0), block_rows)
        key_positions = key_start + jnp.arange(block_rows, dtype=jnp.int32)
        visible = (
            (query_docs[:, None] == key_docs[None, :])
            & (key_positions[None, :] <= positions[:, None])
            & (key_start >= 0)
        )
        needed = (key_start >= 0) & (query_docs[0] == key_docs[block_rows - 1])
        layouts.append((visible, needed))
    start_peak = jnp.full((groups, head_grouping, block_rows), -1e30, jnp.float32)
    start_total = jnp.zeros((groups, head_grouping, block_rows), jnp.float32)
    status = max_update(
        query_half_precision, key_half_precision, layouts[0][0], factor, (start_peak, start_total)
    )
    for offset in range(1, reach + 1):
        status = lax.cond(
            layouts[offset][1],
            partial(
                max_update, query_half_precision, blocks[offset][0], layouts[offset][0], factor
            ),
            unchanged,
            status,
        )
    log_norm = status[0] + jnp.log(status[1])
    row_delta = delta_update(
        query_half_precision,
        key_half_precision,
        values,
        layouts[0][0],
        incoming_gradient_groups,
        log_norm,
        factor,
        jnp.zeros((groups, head_grouping, block_rows), jnp.float32),
    )
    for offset in range(1, reach + 1):
        row_delta = lax.cond(
            layouts[offset][1],
            partial(
                delta_update,
                query_half_precision,
                blocks[offset][0],
                blocks[offset][1],
                layouts[offset][0],
                incoming_gradient_groups,
                log_norm,
                factor,
            ),
            unchanged,
            row_delta,
        )
    query_acc = jnp.zeros((block_rows, groups, head_grouping, head_size), jnp.float32)
    query_acc, own_key, own_value = grad_update(
        query_half_precision,
        key_half_precision,
        values,
        layouts[0][0],
        incoming_gradient_groups,
        log_norm,
        row_delta,
        factor,
        query_acc,
    )
    key_parts = [own_key]
    value_parts = [own_value]
    for offset in range(1, reach + 1):
        query_acc, key_part, value_part = lax.cond(
            layouts[offset][1],
            partial(
                grad_update,
                query_half_precision,
                blocks[offset][0],
                blocks[offset][1],
                layouts[offset][0],
                incoming_gradient_groups,
                log_norm,
                row_delta,
                factor,
            ),
            partial(skip_grads, key_half_precision),
            query_acc,
        )
        key_parts.append(key_part)
        value_parts.append(value_part)
    key_total = key_parts[0]
    value_total = value_parts[0]
    for offset in range(1, reach + 1):
        arrived = (
            from_behind(key_parts[offset].astype(jnp.bfloat16), "ctx", -offset).astype(jnp.float32),
            from_behind(value_parts[offset].astype(jnp.bfloat16), "ctx", -offset).astype(
                jnp.float32
            ),
        )
        key_total = key_total + arrived[0]
        value_total = value_total + arrived[1]
    query_rot_grad = query_acc.reshape(block_rows, query_heads, head_size)
    unused_query, query_pull = jax.vjp(
        lambda inputs, gain_vec: rotate(inputs, gain_vec, positions), query_in, query_gain
    )
    unused_key, key_pull = jax.vjp(
        lambda inputs, gain_vec: rotate(inputs, gain_vec, positions), key_in, key_gain
    )
    query_in_grad, query_gain_part = query_pull(query_rot_grad)
    key_in_grad, key_gain_part = key_pull(key_total)
    gain_sums = lax.psum((query_gain_part, key_gain_part), ("ctx", "tp"))
    rescale = 1.0 / math.sqrt(lax.axis_size("ctx") * block_rows)
    return (
        query_in_grad.astype(jnp.bfloat16),
        key_in_grad.astype(jnp.bfloat16),
        value_total.astype(jnp.bfloat16),
        gain_sums[0] * rescale,
        gain_sums[1] * rescale,
    )


def solution(mesh):
    placed = (
        P("ctx", "tp", None),
        P("ctx", "tp", None),
        P("ctx", "tp", None),
        P(),
        P(),
        P(),
        P("ctx", "tp", None),
    )
    return jax.shard_map(
        on_device,
        mesh=mesh,
        in_specs=placed,
        out_specs=(P("ctx", "tp", None), P("ctx", "tp", None), P("ctx", "tp", None), P(), P()),
        check_vma=False,
    )
```

profile of v0, /device:TPU:0, one launch (start us, length us, event | category | flops | bytes accessed | tf_op | source)
XLA Modules:
  0.0 869.2 jit_solution(605140297353758049)
XLA Ops:
  53.8 11.5 %collective-permute-done.3 = bf16[384,8,128]{2,0,1:T(8,128)(2,1)} collective-permute-done((bf16[384,8,128]{2,0,1:T(8,128)(2,1)}, bf16[384,8,128]{2,0,1:T(8,128)(2,1)}, u32[]{:S(2)}, u32[]{:S(2)}) %collective-permute-start.3) | collective-permute-done | bytes 786464 | tf_op jit(solution)/shard_map/ppermute | solution.py:19
  65.3 29.2 %collective-permute-start.6 = (bf16[384,8,128]{2,0,1:T(8,128)(2,1)}, bf16[384,8,128]{2,0,1:T(8,128)(2,1)}, u32[]{:S(2)}, u32[]{:S(2)}) collective-permute-start(bf16[384,8,128]{2,0,1:T(8,128)(2,1)} %pad_maximum_fusion.1), channel_id=1, source_target_pairs={{0,14},{2,16},{4,18},{6,20},{8,22},{10,24},{12,26},{14,28},{16,30}... | collective-permute-start | bytes 2359304 | tf_op jit(solution)/shard_map/ppermute | solution.py:19
  105.2 18.7 %collective-permute-start.8 = (bf16[384,8,128]{2,0,1:T(8,128)(2,1)}, bf16[384,8,128]{2,0,1:T(8,128)(2,1)}, u32[]{:S(2)}, u32[]{:S(2)}) collective-permute-start(bf16[384,8,128]{2,0,1:T(8,128)(2,1)} %copy.91), channel_id=1, source_target_pairs={{0,2},{2,4},{4,6},{6,8},{8,10},{10,12},{12,14},{14,16},{16,18},{18... | collective-permute-start | bytes 2359304 | tf_op jit(solution)/shard_map/ppermute | solution.py:19
  144.2 8.5 conditional.29
  152.7 70.2 %collective-permute-start.15 = (bf16[384,8,128]{2,0,1:T(8,128)(2,1)}, bf16[384,8,128]{2,0,1:T(8,128)(2,1)}, u32[]{:S(2)}, u32[]{:S(2)}) collective-permute-start(bf16[384,8,128]{2,0,1:T(8,128)(2,1)} %copy.91), channel_id=1, source_target_pairs={{0,16},{2,18},{4,20},{6,22},{8,24},{10,26},{12,28},{14,30},{1,17},... | collective-permute-start | bytes 2359304 | tf_op jit(solution)/shard_map/ppermute | solution.py:19
  222.9 33.7 %collective-permute-start.14 = (bf16[384,8,128]{2,0,1:T(8,128)(2,1)}, bf16[384,8,128]{2,0,1:T(8,128)(2,1)}, u32[]{:S(2)}, u32[]{:S(2)}) collective-permute-start(bf16[384,8,128]{2,0,1:T(8,128)(2,1)} %copy.91), channel_id=1, source_target_pairs={{0,14},{2,16},{4,18},{6,20},{8,22},{10,24},{12,26},{14,28},{16,30}... | collective-permute-start | bytes 2359304 | tf_op jit(solution)/shard_map/ppermute | solution.py:19
  256.6 6.5 collective-permute-start.13
  265.3 44.8 %collective-permute-start.11 = (bf16[384,8,128]{2,0,1:T(8,128)(2,1)}, bf16[384,8,128]{2,0,1:T(8,128)(2,1)}, u32[]{:S(2)}, u32[]{:S(2)}) collective-permute-start(bf16[384,8,128]{2,0,1:T(8,128)(2,1)} %copy.91), channel_id=1, source_target_pairs={{0,8},{2,10},{4,12},{6,14},{8,16},{10,18},{12,20},{14,22},{16,24},... | collective-permute-start | bytes 2359304 | tf_op jit(solution)/shard_map/ppermute | solution.py:19
  310.1 10.9 %fusion.248 = (f32[8,2,384]{2,1,0:T(2,128)S(1)}, f32[8,384,384,2]{2,1,3,0:T(8,128)}) fusion(f32[8,2,384]{2,1,0:T(2,128)S(1)} %bitcast.959, f32[8,384,384,2]{2,1,3,0:T(8,128)} %copy-done.14, pred[384,384]{0,1:T(8,128)(4,1)S(1)} %get-tuple-element.737, bf16[384,8,2,128]{3,0,2,1:T(8,128)(2,1)} %bitcast.932, bf16[384,8,128,1]{2,1,0,3:T(8,128)(2,1)} %bitcast.950), kind=kOutput, calls=%fused_computation.298 | convolution fusion | flops 622848000 | bytes 21430272 | tf_op jit(solution)/shard_map/igrd,jgd->grij/dot_general | solution.py:73
  321.3 8.4 conditional.37
  329.8 8.1 fusion.250
  348.2 6.9 conditional.41
  356.0 6.2 conditional.42
  376.9 6.2 conditional.45
  403.9 107.3 %collective-permute-done.23 = bf16[384,8,128]{2,0,1:T(8,128)(2,1)S(1)} collective-permute-done((bf16[384,8,128]{2,0,1:T(8,128)(2,1)S(1)}, bf16[384,8,128]{2,0,1:T(8,128)(2,1)S(1)}, u32[]{:S(2)}, u32[]{:S(2)}) %collective-permute-start.23) | collective-permute-done | bytes 786464 | tf_op jit(solution)/shard_map/ppermute | solution.py:19
  518.0 18.4 %collective-permute-done.31 = bf16[384,8,128]{2,0,1:T(8,128)(2,1)S(1)} collective-permute-done((bf16[384,8,128]{2,0,1:T(8,128)(2,1)S(1)}, bf16[384,8,128]{2,0,1:T(8,128)(2,1)S(1)}, u32[]{:S(2)}, u32[]{:S(2)}) %collective-permute-start.31) | collective-permute-done | bytes 786464 | tf_op jit(solution)/shard_map/ppermute | solution.py:19
  541.7 34.5 %collective-permute-done.29 = bf16[384,8,128]{2,0,1:T(8,128)(2,1)S(1)} collective-permute-done((bf16[384,8,128]{2,0,1:T(8,128)(2,1)}, bf16[384,8,128]{2,0,1:T(8,128)(2,1)S(1)}, u32[]{:S(2)}, u32[]{:S(2)}) %collective-permute-start.29) | collective-permute-done | bytes 786464 | tf_op jit(solution)/shard_map/ppermute | solution.py:19
  585.6 6.3 fusion.256
  593.2 43.6 %collective-permute-done.27 = bf16[384,8,128]{2,0,1:T(8,128)(2,1)} collective-permute-done((bf16[384,8,128]{2,0,1:T(8,128)(2,1)}, bf16[384,8,128]{2,0,1:T(8,128)(2,1)}, u32[]{:S(2)}, u32[]{:S(2)}) %collective-permute-start.27) | collective-permute-done | bytes 786464 | tf_op jit(solution)/shard_map/ppermute | solution.py:19
  639.3 10.5 %collective-permute-done.25 = bf16[384,8,128]{2,0,1:T(8,128)(2,1)} collective-permute-done((bf16[384,8,128]{2,0,1:T(8,128)(2,1)}, bf16[384,8,128]{2,0,1:T(8,128)(2,1)}, u32[]{:S(2)}, u32[]{:S(2)}) %collective-permute-start.25) | collective-permute-done | bytes 786464 | tf_op jit(solution)/shard_map/ppermute | solution.py:19
  653.1 8.8 %fusion.272 = bf16[384,8,128]{2,0,1:T(8,128)(2,1)S(1)} fusion(bf16[384,8,128]{2,0,1:T(8,128)(2,1)} %copy-done.96, bf16[384,8,128]{2,0,1:T(8,128)(2,1)} %copy-done.97, bf16[384,8,128]{2,0,1:T(8,128)(2,1)} %copy-done.98, bf16[384,8,128]{2,0,1:T(8,128)(2,1)} %collective-permute-done.28, bf16[384,8,128]{2,0,1:T(8,128)(2,1)} %collective-permute-done.27, ...), kind=kOutput, calls=%fused_computation.343 | convolution fusion | flops 622460928 | bytes 18259968 | tf_op jit(solution)/shard_map/grij,igrd->jgd/dot_general | solution.py:128
  663.3 38.4 %collective-permute-done.20 = bf16[384,8,128]{2,0,1:T(8,128)(2,1)S(1)} collective-permute-done((bf16[384,8,128]{2,0,1:T(8,128)(2,1)S(1)}, bf16[384,8,128]{2,0,1:T(8,128)(2,1)S(1)}, u32[]{:S(2)}, u32[]{:S(2)}) %collective-permute-start.20) | collective-permute-done | bytes 786464 | tf_op jit(solution)/shard_map/ppermute | solution.py:19
  701.7 21.9 %collective-permute-done.19 = bf16[384,8,128]{2,0,1:T(8,128)(2,1)S(1)} collective-permute-done((bf16[384,8,128]{2,0,1:T(8,128)(2,1)S(1)}, bf16[384,8,128]{2,0,1:T(8,128)(2,1)S(1)}, u32[]{:S(2)}, u32[]{:S(2)}) %collective-permute-start.19) | collective-permute-done | bytes 786464 | tf_op jit(solution)/shard_map/ppermute | solution.py:19
  730.9 136.8 %all-reduce.4 = (f32[128]{0:T(128)S(1)}, f32[128]{0:T(128)S(1)}) all-reduce(f32[128]{0:T(128)S(1)} %get-tuple-element.692, f32[128]{0:T(128)S(1)} %get-tuple-element.694), channel_id=1, replica_groups=mesh['ctx'=16,'tp'=2] {'ctx','tp'}, use_global_device_ids=true, to_apply=%region_80.81 | all-reduce | flops 256 | bytes 2048 | tf_op jit(solution)/shard_map/psum | solution.py:268
  (255 shorter events, 170.8 us)
Async XLA Ops:
  20.4 77.1 %collective-permute-start.2 = (bf16[384,8,128]{2,0,1:T(8,128)(2,1)}, bf16[384,8,128]{2,0,1:T(8,128)(2,1)}, u32[]{:S(2)}, u32[]{:S(2)}) collective-permute-start(bf16[384,8,128]{2,0,1:T(8,128)(2,1)} %pad_maximum_fusion.1), channel_id=1, source_target_pairs={{0,6},{2,8},{4,10},{6,12},{8,14},{10,16},{12,18},{14,20},{16,22},{... | collective-permute-start | bytes 2359304 | tf_op jit(solution)/shard_map/ppermute | solution.py:19
  24.1 78.9 %collective-permute-start.1 = (bf16[384,8,128]{2,0,1:T(8,128)(2,1)}, bf16[384,8,128]{2,0,1:T(8,128)(2,1)}, u32[]{:S(2)}, u32[]{:S(2)}) collective-permute-start(bf16[384,8,128]{2,0,1:T(8,128)(2,1)} %pad_maximum_fusion.1), channel_id=1, source_target_pairs={{0,4},{2,6},{4,8},{6,10},{8,12},{10,14},{12,16},{14,18},{16,20},{1... | collective-permute-start | bytes 2359304 | tf_op jit(solution)/shard_map/ppermute | solution.py:19
  50.5 172.4 %collective-permute-start.7 = (bf16[384,8,128]{2,0,1:T(8,128)(2,1)}, bf16[384,8,128]{2,0,1:T(8,128)(2,1)}, u32[]{:S(2)}, u32[]{:S(2)}) collective-permute-start(bf16[384,8,128]{2,0,1:T(8,128)(2,1)} %pad_maximum_fusion.1), channel_id=1, source_target_pairs={{0,16},{2,18},{4,20},{6,22},{8,24},{10,26},{12,28},{14,30},{1,17},... | collective-permute-start | bytes 2359304 | tf_op jit(solution)/shard_map/ppermute | solution.py:19
  65.3 87.5 %collective-permute-start.6 = (bf16[384,8,128]{2,0,1:T(8,128)(2,1)}, bf16[384,8,128]{2,0,1:T(8,128)(2,1)}, u32[]{:S(2)}, u32[]{:S(2)}) collective-permute-start(bf16[384,8,128]{2,0,1:T(8,128)(2,1)} %pad_maximum_fusion.1), channel_id=1, source_target_pairs={{0,14},{2,16},{4,18},{6,20},{8,22},{10,24},{12,26},{14,28},{16,30}... | collective-permute-start | bytes 2359304 | tf_op jit(solution)/shard_map/ppermute | solution.py:19
  97.5 159.1 %collective-permute-start.10 = (bf16[384,8,128]{2,0,1:T(8,128)(2,1)}, bf16[384,8,128]{2,0,1:T(8,128)(2,1)}, u32[]{:S(2)}, u32[]{:S(2)}) collective-permute-start(bf16[384,8,128]{2,0,1:T(8,128)(2,1)} %copy.91), channel_id=1, source_target_pairs={{0,6},{2,8},{4,10},{6,12},{8,14},{10,16},{12,18},{14,20},{16,22},{... | collective-permute-start | bytes 2359304 | tf_op jit(solution)/shard_map/ppermute | solution.py:19
  103.0 160.1 %collective-permute-start.9 = (bf16[384,8,128]{2,0,1:T(8,128)(2,1)}, bf16[384,8,128]{2,0,1:T(8,128)(2,1)}, u32[]{:S(2)}, u32[]{:S(2)}) collective-permute-start(bf16[384,8,128]{2,0,1:T(8,128)(2,1)} %copy.91), channel_id=1, source_target_pairs={{0,4},{2,6},{4,8},{6,10},{8,12},{10,14},{12,16},{14,18},{16,20},{1... | collective-permute-start | bytes 2359304 | tf_op jit(solution)/shard_map/ppermute | solution.py:19
  105.2 160.1 %collective-permute-start.8 = (bf16[384,8,128]{2,0,1:T(8,128)(2,1)}, bf16[384,8,128]{2,0,1:T(8,128)(2,1)}, u32[]{:S(2)}, u32[]{:S(2)}) collective-permute-start(bf16[384,8,128]{2,0,1:T(8,128)(2,1)} %copy.91), channel_id=1, source_target_pairs={{0,2},{2,4},{4,6},{6,8},{8,10},{10,12},{12,14},{14,16},{16,18},{18... | collective-permute-start | bytes 2359304 | tf_op jit(solution)/shard_map/ppermute | solution.py:19
  152.7 177.1 %collective-permute-start.15 = (bf16[384,8,128]{2,0,1:T(8,128)(2,1)}, bf16[384,8,128]{2,0,1:T(8,128)(2,1)}, u32[]{:S(2)}, u32[]{:S(2)}) collective-permute-start(bf16[384,8,128]{2,0,1:T(8,128)(2,1)} %copy.91), channel_id=1, source_target_pairs={{0,16},{2,18},{4,20},{6,22},{8,24},{10,26},{12,28},{14,30},{1,17},... | collective-permute-start | bytes 2359304 | tf_op jit(solution)/shard_map/ppermute | solution.py:19
  222.9 106.9 %collective-permute-start.14 = (bf16[384,8,128]{2,0,1:T(8,128)(2,1)}, bf16[384,8,128]{2,0,1:T(8,128)(2,1)}, u32[]{:S(2)}, u32[]{:S(2)}) collective-permute-start(bf16[384,8,128]{2,0,1:T(8,128)(2,1)} %copy.91), channel_id=1, source_target_pairs={{0,14},{2,16},{4,18},{6,20},{8,22},{10,24},{12,26},{14,28},{16,30}... | collective-permute-start | bytes 2359304 | tf_op jit(solution)/shard_map/ppermute | solution.py:19
  397.3 113.9 %collective-permute-start.23 = (bf16[384,8,128]{2,0,1:T(8,128)(2,1)S(1)}, bf16[384,8,128]{2,0,1:T(8,128)(2,1)S(1)}, u32[]{:S(2)}, u32[]{:S(2)}) collective-permute-start(bf16[384,8,128]{2,0,1:T(8,128)(2,1)S(1)} %get-tuple-element.638), channel_id=1, source_target_pairs={{16,0},{18,2},{20,4},{22,6},{24,8},{26,10},{28,12},{30,14},{17,1},... | collective-permute-start | bytes 2359304 | tf_op jit(solution)/shard_map/ppermute | solution.py:19
  398.7 137.8 %collective-permute-start.31 = (bf16[384,8,128]{2,0,1:T(8,128)(2,1)S(1)}, bf16[384,8,128]{2,0,1:T(8,128)(2,1)S(1)}, u32[]{:S(2)}, u32[]{:S(2)}) collective-permute-start(bf16[384,8,128]{2,0,1:T(8,128)(2,1)S(1)} %get-tuple-element.646), channel_id=1, source_target_pairs={{16,0},{18,2},{20,4},{22,6},{24,8},{26,10},{28,12},{30,14},{17,1},... | collective-permute-start | bytes 2359304 | tf_op jit(solution)/shard_map/ppermute | solution.py:19
  400.0 137.7 %collective-permute-start.22 = (bf16[384,8,128]{2,0,1:T(8,128)(2,1)}, bf16[384,8,128]{2,0,1:T(8,128)(2,1)S(1)}, u32[]{:S(2)}, u32[]{:S(2)}) collective-permute-start(bf16[384,8,128]{2,0,1:T(8,128)(2,1)} %copy-done.87), channel_id=1, source_target_pairs={{14,0},{16,2},{18,4},{20,6},{22,8},{24,10},{26,12},{28,14},{30,16}... | collective-permute-start | bytes 2359304 | tf_op jit(solution)/shard_map/ppermute | solution.py:19
  401.3 137.8 %collective-permute-start.30 = (bf16[384,8,128]{2,0,1:T(8,128)(2,1)}, bf16[384,8,128]{2,0,1:T(8,128)(2,1)S(1)}, u32[]{:S(2)}, u32[]{:S(2)}) collective-permute-start(bf16[384,8,128]{2,0,1:T(8,128)(2,1)} %copy-done.86), channel_id=1, source_target_pairs={{14,0},{16,2},{18,4},{20,6},{22,8},{24,10},{26,12},{28,14},{30,16}... | collective-permute-start | bytes 2359304 | tf_op jit(solution)/shard_map/ppermute | solution.py:19
  402.6 137.8 %collective-permute-start.21 = (bf16[384,8,128]{2,0,1:T(8,128)(2,1)}, bf16[384,8,128]{2,0,1:T(8,128)(2,1)S(1)}, u32[]{:S(2)}, u32[]{:S(2)}) collective-permute-start(bf16[384,8,128]{2,0,1:T(8,128)(2,1)} %copy-done.85), channel_id=1, source_target_pairs={{12,0},{14,2},{16,4},{18,6},{20,8},{22,10},{24,12},{26,14},{28,16}... | collective-permute-start | bytes 2359304 | tf_op jit(solution)/shard_map/ppermute | solution.py:19
  511.2 65.0 %collective-permute-start.29 = (bf16[384,8,128]{2,0,1:T(8,128)(2,1)}, bf16[384,8,128]{2,0,1:T(8,128)(2,1)S(1)}, u32[]{:S(2)}, u32[]{:S(2)}) collective-permute-start(bf16[384,8,128]{2,0,1:T(8,128)(2,1)} %copy-done.84), channel_id=1, source_target_pairs={{12,0},{14,2},{16,4},{18,6},{20,8},{22,10},{24,12},{26,14},{28,16}... | collective-permute-start | bytes 2359304 | tf_op jit(solution)/shard_map/ppermute | solution.py:19
  537.8 99.0 %collective-permute-start.27 = (bf16[384,8,128]{2,0,1:T(8,128)(2,1)}, bf16[384,8,128]{2,0,1:T(8,128)(2,1)}, u32[]{:S(2)}, u32[]{:S(2)}) collective-permute-start(bf16[384,8,128]{2,0,1:T(8,128)(2,1)} %get-tuple-element.642), channel_id=1, source_target_pairs={{8,0},{10,2},{12,4},{14,6},{16,8},{18,10},{20,12},{22,14},{24,16},... | collective-permute-start | bytes 2359304 | tf_op jit(solution)/shard_map/ppermute | solution.py:19
  539.1 98.9 %collective-permute-start.26 = (bf16[384,8,128]{2,0,1:T(8,128)(2,1)}, bf16[384,8,128]{2,0,1:T(8,128)(2,1)}, u32[]{:S(2)}, u32[]{:S(2)}) collective-permute-start(bf16[384,8,128]{2,0,1:T(8,128)(2,1)} %get-tuple-element.641), channel_id=1, source_target_pairs={{6,0},{8,2},{10,4},{12,6},{14,8},{16,10},{18,12},{20,14},{22,16},{... | collective-permute-start | bytes 2359304 | tf_op jit(solution)/shard_map/ppermute | solution.py:19
  540.4 109.5 %collective-permute-start.25 = (bf16[384,8,128]{2,0,1:T(8,128)(2,1)}, bf16[384,8,128]{2,0,1:T(8,128)(2,1)}, u32[]{:S(2)}, u32[]{:S(2)}) collective-permute-start(bf16[384,8,128]{2,0,1:T(8,128)(2,1)} %get-tuple-element.640), channel_id=1, source_target_pairs={{4,0},{6,2},{8,4},{10,6},{12,8},{14,10},{16,12},{18,14},{20,16},{2... | collective-permute-start | bytes 2359304 | tf_op jit(solution)/shard_map/ppermute | solution.py:19
  576.2 75.0 %collective-permute-start.24 = (bf16[384,8,128]{2,0,1:T(8,128)(2,1)}, bf16[384,8,128]{2,0,1:T(8,128)(2,1)}, u32[]{:S(2)}, u32[]{:S(2)}) collective-permute-start(bf16[384,8,128]{2,0,1:T(8,128)(2,1)} %get-tuple-element.639), channel_id=1, source_target_pairs={{2,0},{4,2},{6,4},{8,6},{10,8},{12,10},{14,12},{16,14},{18,16},{20... | collective-permute-start | bytes 2359304 | tf_op jit(solution)/shard_map/ppermute | solution.py:19
  591.9 109.8 %collective-permute-start.20 = (bf16[384,8,128]{2,0,1:T(8,128)(2,1)S(1)}, bf16[384,8,128]{2,0,1:T(8,128)(2,1)S(1)}, u32[]{:S(2)}, u32[]{:S(2)}) collective-permute-start(bf16[384,8,128]{2,0,1:T(8,128)(2,1)S(1)} %copy-done.83), channel_id=1, source_target_pairs={{10,0},{12,2},{14,4},{16,6},{18,8},{20,10},{22,12},{24,14},{26,16}... | collective-permute-start | bytes 2359304 | tf_op jit(solution)/shard_map/ppermute | solution.py:19
  636.7 86.9 %collective-permute-start.19 = (bf16[384,8,128]{2,0,1:T(8,128)(2,1)S(1)}, bf16[384,8,128]{2,0,1:T(8,128)(2,1)S(1)}, u32[]{:S(2)}, u32[]{:S(2)}) collective-permute-start(bf16[384,8,128]{2,0,1:T(8,128)(2,1)S(1)} %copy-done.81), channel_id=1, source_target_pairs={{8,0},{10,2},{12,4},{14,6},{16,8},{18,10},{20,12},{22,14},{24,16},... | collective-permute-start | bytes 2359304 | tf_op jit(solution)/shard_map/ppermute | solution.py:19
  638.0 85.6 %collective-permute-start.18 = (bf16[384,8,128]{2,0,1:T(8,128)(2,1)S(1)}, bf16[384,8,128]{2,0,1:T(8,128)(2,1)S(1)}, u32[]{:S(2)}, u32[]{:S(2)}) collective-permute-start(bf16[384,8,128]{2,0,1:T(8,128)(2,1)S(1)} %copy-done.79), channel_id=1, source_target_pairs={{6,0},{8,2},{10,4},{12,6},{14,8},{16,10},{18,12},{20,14},{22,16},{... | collective-permute-start | bytes 2359304 | tf_op jit(solution)/shard_map/ppermute | solution.py:19
  649.9 73.7 %collective-permute-start.17 = (bf16[384,8,128]{2,0,1:T(8,128)(2,1)S(1)}, bf16[384,8,128]{2,0,1:T(8,128)(2,1)S(1)}, u32[]{:S(2)}, u32[]{:S(2)}) collective-permute-start(bf16[384,8,128]{2,0,1:T(8,128)(2,1)S(1)} %copy-done.77), channel_id=1, source_target_pairs={{4,0},{6,2},{8,4},{10,6},{12,8},{14,10},{16,12},{18,14},{20,16},{2... | collective-permute-start | bytes 2359304 | tf_op jit(solution)/shard_map/ppermute | solution.py:19
  651.2 72.4 %collective-permute-start.16 = (bf16[384,8,128]{2,0,1:T(8,128)(2,1)}, bf16[384,8,128]{2,0,1:T(8,128)(2,1)S(1)}, u32[]{:S(2)}, u32[]{:S(2)}) collective-permute-start(bf16[384,8,128]{2,0,1:T(8,128)(2,1)} %get-tuple-element.631), channel_id=1, source_target_pairs={{2,0},{4,2},{6,4},{8,6},{10,8},{12,10},{14,12},{16,14},{18,16},{20... | collective-permute-start | bytes 2359304 | tf_op jit(solution)/shard_map/ppermute | solution.py:19
  (64 other events, 2798.9 us)
where the time goes:
time: 880 us; the launch traced here: 869 us
  waiting for transfers between devices  286 us (32%)
  starting transfers between devices  260 us (30%)
  blocking collectives  137 us (16%)
  loops' own time  55.6 us (6%)
  other arithmetic  46.7 us (5%)
  local copies, waits for them, and re-layouts  42.8 us (5%)
  matrix products  28.6 us (3%)
  between operations  12.9 us (1%)
    ppermute x32, waiting for transfers between devices, from_behind(): lax.ppermute(value, axis, [(source, source + steps) for source in range(f...  286 us
    ppermute x32, starting transfers between devices, from_behind(): lax.ppermute(value, axis, [(source, source + steps) for source in range(f...  260 us
    psum x1, blocking collectives, on_device(): gain_sums = lax.psum((query_gain_part, key_gain_part), ('ctx', 'tp'))  137 us
    another operation x8, loops' own time, on_device(): lax.cond(layouts[offset][1], partial(grad_update, query_half_precision, b...  38.2 us
  transfers between devices with their start and end apart: 32, of which 8 were waited for; matrix products, arithmetic and copies ran while one was open for 9% of the time, Pallas kernels for 0%

commit v1 on v0

v1 whole, which is shorter than its diff:
```python
from functools import partial
import math

import jax
import jax.numpy as jnp
from jax import lax
from jax.experimental import pallas as pl
from jax.experimental.pallas import tpu as pltpu
from jax.sharding import PartitionSpec as P

QUERY_SCALAR = 168
REACH = 8
CHUNKS = 4

rope_base = 1000000.0
norm_eps = 1e-06
HIDDEN = -1e30
LOG2E = 1.4426950408889634


def tables(positions, head_size):
    half_dim = head_size // 2
    inverse_freq = rope_base ** (-2.0 * jnp.arange(half_dim, dtype=jnp.float32) / head_size)
    angles = positions.astype(jnp.float32)[:, None] * inverse_freq[None, :]
    return lax.optimization_barrier((jnp.cos(angles), jnp.sin(angles)))


def rotate(inputs, gain_vec, cosine, sine_part):
    meansq = jnp.mean(inputs * inputs, axis=-1, keepdims=True)
    normed = inputs * lax.rsqrt(meansq + norm_eps) * gain_vec
    half_dim = inputs.shape[-1] // 2
    leading = normed[..., :half_dim]
    trailing = normed[..., half_dim:]
    return jnp.concatenate(
        [leading * cosine - trailing * sine_part, trailing * cosine + leading * sine_part], axis=-1
    )


def dot(a, b, dims):
    return lax.dot_general(a, b, (dims, ((), ())), preferred_element_type=jnp.float32)


def attend_kernel(
    factor,
    width,
    info,
    q_ref,
    up_ref,
    k_ref,
    v_ref,
    begin_ref,
    place_ref,
    dq_ref,
    dk_ref,
    dv_ref,
    held_p,
    held_dp,
    held_peak,
    peak_ref,
    total_ref,
    delta_ref,
    dq_acc,
):
    first, own, clear = info[0], info[1], info[2]
    blocks, _, rows, _ = k_ref.shape
    lanes = q_ref.shape[1]
    parts = [pl.ds(at, width) for at in range(0, lanes, width)]
    peak_ref[...] = jnp.full(peak_ref.shape, HIDDEN, jnp.float32)
    total_ref[...] = jnp.zeros(total_ref.shape, jnp.float32)
    delta_ref[...] = jnp.zeros(delta_ref.shape, jnp.float32)
    dq_acc[...] = jnp.zeros(dq_acc.shape, jnp.float32)

    @pl.loop(0, blocks)
    def _(block):
        @pl.when((block < first) | (block > own))
        def _():
            dk_ref[block, 0] = jnp.zeros(dk_ref.shape[2:], dk_ref.dtype)
            dv_ref[block, 0] = jnp.zeros(dv_ref.shape[2:], dv_ref.dtype)

    def forward(block, masked):
        slot = block - first
        key_blk = k_ref[block, 0]
        value_blk = v_ref[block, 0]
        for part in parts:
            scores = dot(key_blk, q_ref[0, part, :], ((1,), (1,))) * (factor * LOG2E)
            attend_grad = dot(value_blk, up_ref[0, part, :], ((1,), (1,)))
            if masked:
                key_at = block * rows + lax.broadcasted_iota(jnp.int32, scores.shape, 0)
                seen = (key_at >= begin_ref[:, part]) & (key_at <= place_ref[:, part])
                scores = jnp.where(seen, scores, HIDDEN)
            old_peak = peak_ref[:, part]
            peak = jnp.maximum(old_peak, jnp.max(scores, axis=0, keepdims=True))
            grown = jnp.exp2(scores - peak)
            shrink = jnp.exp2(old_peak - peak)
            total_ref[:, part] = total_ref[:, part] * shrink + jnp.sum(grown, axis=0, keepdims=True)
            delta_ref[:, part] = delta_ref[:, part] * shrink + jnp.sum(
                grown * attend_grad, axis=0, keepdims=True
            )
            peak_ref[:, part] = peak
            held_peak[slot, :, part] = peak
            held_p[slot, :, part] = grown
            held_dp[slot, :, part] = attend_grad

    @pl.loop(first, own + 1)
    def _(block):
        inside = (block >= clear) & (block < own)

        @pl.when(inside)
        def _():
            forward(block, False)

        @pl.when(jnp.logical_not(inside))
        def _():
            forward(block, True)

    total_ref[...] = 1.0 / total_ref[...]
    delta_ref[...] = delta_ref[...] * total_ref[...]

    @pl.loop(first, own + 1)
    def _(block):
        slot = block - first
        turned_key = k_ref[block, 0].T
        dk = jnp.zeros(dk_ref.shape[2:], jnp.float32)
        dv = jnp.zeros(dv_ref.shape[2:], jnp.float32)
        for part in parts:
            weight = jnp.exp2(held_peak[slot, :, part] - peak_ref[:, part]) * total_ref[:, part]
            attend = held_p[slot, :, part] * weight
            score_grad = (attend * (held_dp[slot, :, part] - delta_ref[:, part])).astype(jnp.bfloat16)
            dv = dv + dot(attend.astype(jnp.bfloat16), up_ref[0, part, :], ((1,), (0,)))
            dk = dk + dot(score_grad, q_ref[0, part, :], ((1,), (0,)))
            dq_acc[:, part] += dot(turned_key, score_grad, ((1,), (0,)))
        dk_ref[block, 0] = (dk * factor).astype(dk_ref.dtype)
        dv_ref[block, 0] = dv.astype(dv_ref.dtype)

    dq_ref[0] = dq_acc[...].T * factor


def attend_grads(info, query_rot, upstream, keys, values, begin, place, reach, factor):
    groups, lanes, head_size = query_rot.shape
    blocks, _, rows, _ = keys.shape
    width = 256 if lanes % 256 == 0 else lanes
    slots = min(reach + 1, blocks)
    own_spec = pl.BlockSpec((1, lanes, head_size), lambda g, info: (g, 0, 0))
    all_spec = pl.BlockSpec((blocks, 1, rows, head_size), lambda g, info: (0, g, 0, 0))
    row_spec = pl.BlockSpec((1, lanes), lambda g, info: (0, 0))
    pairs = groups * lanes * rows * (slots // 2 + 1)
    return pl.pallas_call(
        partial(attend_kernel, factor, width),
        grid_spec=pltpu.PrefetchScalarGridSpec(
            num_scalar_prefetch=1,
            grid=(groups,),
            in_specs=[own_spec, own_spec, all_spec, all_spec, row_spec, row_spec],
            out_specs=[own_spec, all_spec, all_spec],
            scratch_shapes=[
                pltpu.VMEM((slots, rows, lanes), jnp.float32),
                pltpu.VMEM((slots, rows, lanes), jnp.float32),
                pltpu.VMEM((slots, 1, lanes), jnp.float32),
                pltpu.VMEM((1, lanes), jnp.float32),
                pltpu.VMEM((1, lanes), jnp.float32),
                pltpu.VMEM((1, lanes), jnp.float32),
                pltpu.VMEM((head_size, lanes), jnp.float32),
            ],
        ),
        out_shape=(
            jax.ShapeDtypeStruct(query_rot.shape, jnp.float32),
            jax.ShapeDtypeStruct(keys.shape, jnp.bfloat16),
            jax.ShapeDtypeStruct(keys.shape, jnp.bfloat16),
        ),
        compiler_params=pltpu.CompilerParams(
            dimension_semantics=("arbitrary",), vmem_limit_bytes=58 * 1024 * 1024
        ),
        cost_estimate=pl.CostEstimate(
            flops=20 * pairs * head_size,
            transcendentals=pairs,
            bytes_accessed=8 * keys.size + 8 * query_rot.size,
        ),
    )(info, query_rot, upstream, keys, values, begin, place)


def on_device(query_raw, key_raw, values, query_gain, key_gain, documents, upstream):
    block_rows, query_heads, head_size = query_raw.shape
    groups = key_raw.shape[1]
    head_grouping = query_heads // groups
    lanes = head_grouping * block_rows
    factor = QUERY_SCALAR ** (-0.5)
    reach = min(REACH, lax.axis_size("ctx") // 2)
    own = lax.axis_index("ctx").astype(jnp.int32)
    first_row = own * block_rows
    positions = first_row + jnp.arange(block_rows, dtype=jnp.int32)
    cosine, sine_part = tables(positions, head_size)
    chunks = math.gcd(CHUNKS, groups)
    size = groups // chunks

    key_in = jnp.swapaxes(key_raw, 0, 1).astype(jnp.float32)
    key_rot = rotate(key_in, key_gain, cosine, sine_part).astype(jnp.bfloat16)
    value_turned = jnp.swapaxes(values, 0, 1)
    gathered = [
        lax.all_gather(
            jnp.stack([key_rot[at : at + size], value_turned[at : at + size]]), "ctx", axis=0
        )
        for at in range(0, groups, size)
    ]
    query_in = jnp.swapaxes(query_raw, 0, 1).astype(jnp.float32)
    query_rot = (
        rotate(query_in, query_gain, cosine, sine_part)
        .astype(jnp.bfloat16)
        .reshape(groups, lanes, head_size)
    )
    upstream_turned = jnp.swapaxes(upstream, 0, 1).reshape(groups, lanes, head_size)

    own_docs = lax.dynamic_slice_in_dim(documents, first_row, block_rows)
    begin = jnp.sum((documents[None, :] < own_docs[:, None]).astype(jnp.int32), axis=1)
    info = jnp.stack(
        [
            jnp.maximum(begin[0] // block_rows, own - reach),
            own,
            (begin[-1] + block_rows - 1) // block_rows,
        ]
    ).astype(jnp.int32)
    begin_row = jnp.tile(begin, head_grouping)[None, :]
    place_row = jnp.tile(positions, head_grouping)[None, :]

    dq, dk, dv = [], [], []
    for index in range(chunks):
        at = index * size
        dq_part, dk_part, dv_part = attend_grads(
            info,
            query_rot[at : at + size],
            upstream_turned[at : at + size],
            gathered[index][:, 0],
            gathered[index][:, 1],
            begin_row,
            place_row,
            reach,
            factor,
        )
        dq.append(dq_part)
        dk.append(lax.psum_scatter(dk_part, "ctx", scatter_dimension=0))
        dv.append(lax.psum_scatter(dv_part, "ctx", scatter_dimension=0))
    query_rot_grad = jnp.concatenate(dq).reshape(query_heads, block_rows, head_size)
    key_total = jnp.concatenate(dk).astype(jnp.float32)
    value_total = jnp.concatenate(dv)

    turn = lambda inputs, gain_vec: rotate(inputs, gain_vec, cosine, sine_part)
    _, query_pull = jax.vjp(turn, query_in, query_gain)
    _, key_pull = jax.vjp(turn, key_in, key_gain)
    query_in_grad, query_gain_part = query_pull(query_rot_grad)
    key_in_grad, key_gain_part = key_pull(key_total)
    gain_sums = lax.psum(jnp.stack([query_gain_part, key_gain_part]), ("ctx", "tp"))
    rescale = 1.0 / math.sqrt(lax.axis_size("ctx") * block_rows)
    return (
        jnp.swapaxes(query_in_grad.astype(jnp.bfloat16), 0, 1),
        jnp.swapaxes(key_in_grad.astype(jnp.bfloat16), 0, 1),
        jnp.swapaxes(value_total, 0, 1),
        gain_sums[0] * rescale,
        gain_sums[1] * rescale,
    )


def solution(mesh):
    placed = (
        P("ctx", "tp", None),
        P("ctx", "tp", None),
        P("ctx", "tp", None),
        P(),
        P(),
        P(),
        P("ctx", "tp", None),
    )
    return jax.shard_map(
        on_device,
        mesh=mesh,
        in_specs=placed,
        out_specs=(P("ctx", "tp", None), P("ctx", "tp", None), P("ctx", "tp", None), P(), P()),
        check_vma=False,
    )
```

time: 880 us -> 833 us (0.947); the launches traced: 869 us -> 832 us
  waiting for transfers between devices: 286 us -> 659 us
  starting transfers between devices: 260 us -> 0.89 us
  blocking collectives: 137 us -> 40.6 us
  loops' own time: 55.6 us -> 0 us
  Pallas kernels: 0 us -> 35.4 us
  matrix products: 28.6 us -> 0 us
  other arithmetic: 46.7 us -> 35.1 us
    reduce_scatter x0 -> x8, waiting for transfers between devices: none -> 470 us  [the longest x4 238 us: on_device(): dk.append(lax.psum_scatter(dk_part, 'ctx', scatter_dimension=0))]
    ppermute x32 -> x0, waiting for transfers between devices: 286 us -> none  [from_behind(): lax.ppermute(value, axis, [(source, source + steps) for source in range(f...]
    ppermute x32 -> x0, starting transfers between devices: 260 us -> none  [from_behind(): lax.ppermute(value, axis, [(source, source + steps) for source in range(f...]
    all_gather x0 -> x4, waiting for transfers between devices: none -> 186 us  [on_device(): lax.all_gather(jnp.stack([key_rot[at:at + size], value_turned[at:at + siz...]
    psum x1, blocking collectives: 137 us -> 40.6 us  [on_device(): lax.psum(jnp.stack([query_gain_part, key_gain_part]), ('ctx', 'tp'))]
    another operation x24 -> x0, loops' own time: 55.6 us -> none  [the longest x8 38.2 us: on_device(): lax.cond(layouts[offset][1], partial(grad_update, query_half_precision, b...]
    pallas_call x0 -> x4, Pallas kernels: none -> 35.4 us  [attend_grads(): pl.pallas_call(partial(attend_kernel, factor, width), grid_spec=pltpu.Pre...]
    dot_general x5 -> x0, matrix products: 28.6 us -> none  [the longest x1 10.9 us: block_attend(): jnp.einsum('igrd,jgd->grij', incoming_gradient_groups, value_bf, preferre...]
  transfers between devices with their start and end apart: 32 -> 12, of which waited for: 8 -> 12; matrix products, arithmetic and copies ran while one was open for 9% -> 8% of each run, Pallas kernels for 0% -> 4%
where the time goes in v1:
time: 833 us; the launch traced here: 832 us
  waiting for transfers between devices  659 us (79%)
  local copies, waits for them, and re-layouts  44.3 us (5%)
  blocking collectives  40.6 us (5%)
  Pallas kernels  35.4 us (4%)
  other arithmetic  35.1 us (4%)
  between operations  17.2 us (2%)
    reduce_scatter x4, waiting for transfers between devices, on_device(): dk.append(lax.psum_scatter(dk_part, 'ctx', scatter_dimension=0))  238 us
    reduce_scatter x4, waiting for transfers between devices, on_device(): dv.append(lax.psum_scatter(dv_part, 'ctx', scatter_dimension=0))  232 us
    all_gather x4, waiting for transfers between devices, on_device(): lax.all_gather(jnp.stack([key_rot[at:at + size], value_turned[at:at + siz...  186 us
    psum x1, blocking collectives, on_device(): lax.psum(jnp.stack([query_gain_part, key_gain_part]), ('ctx', 'tp'))  40.6 us
    pallas_call x4, Pallas kernels, attend_grads(): pl.pallas_call(partial(attend_kernel, factor, width), grid_spec=pltpu.Pre...  35.4 us
    squeeze x4, local copies, waits for them, and re-layouts, on_device(): gathered[index][:, 1]  25.1 us
  transfers between devices with their start and end apart: 12, of which 12 were waited for; matrix products, arithmetic and copies ran while one was open for 8% of the time, Pallas kernels for 4%

profile of v1, /device:TPU:0, one launch (start us, length us, event | category | flops | bytes accessed | tf_op | source)
XLA Modules:
  0.0 832.3 jit_solution(15573175145068719510)
XLA Ops:
  30.1 48.2 %all-gather.9.cloned.1.call-done = bf16[32,2,384,128]{3,2,1,0:T(8,128)(2,1)} async-done(((bf16[2,2,384,128]{3,2,1,0:T(8,128)(2,1)}), bf16[32,2,384,128]{3,2,1,0:T(8,128)(2,1)}) %all-gather.9.cloned.1.call-update) | async-done | bytes 6291472 | tf_op jit(solution)/shard_map/all_gather | solution.py:198
  78.3 6.3 slice_bitcast_fusion.6
  84.6 8.9 %shard_map.110 = (f32[2,768,128]{2,1,0:T(8,128)}, bf16[16,2,384,128]{3,2,1,0:T(8,128)(2,1)}, bf16[16,2,384,128]{3,2,1,0:T(8,128)(2,1)}) custom-call(s32[3]{0:T(128)} %pad_add_fusion.2.info, bf16[2,768,128]{2,1,0:T(8,128)(2,1)} %bitcast.145, bf16[2,768,128]{2,1,0:T(8,128)(2,1)} %bitcast.146, bf16[16,2,384,128]{3,2,1,0:T(8,128)(2,1)} %get-tuple-element.75.k_ref, ...), custom_call_target="tpu_custom_call" | custom-call | flops 7549747200 | bytes 14155776 | tf_op jit(solution)/shard_map/pallas_call | solution.py:147
  95.3 46.0 %all-gather.11.cloned.1.call-done = bf16[32,2,384,128]{3,2,1,0:T(8,128)(2,1)} async-done(((bf16[2,2,384,128]{3,2,1,0:T(8,128)(2,1)}), bf16[32,2,384,128]{3,2,1,0:T(8,128)(2,1)}) %all-gather.11.cloned.1.call-update) | async-done | bytes 6291472 | tf_op jit(solution)/shard_map/all_gather | solution.py:198
  141.3 6.3 slice_bitcast_fusion.4
  147.6 8.8 %shard_map.111 = (f32[2,768,128]{2,1,0:T(8,128)}, bf16[16,2,384,128]{3,2,1,0:T(8,128)(2,1)}, bf16[16,2,384,128]{3,2,1,0:T(8,128)(2,1)}) custom-call(s32[3]{0:T(128)} %pad_add_fusion.2.info, bf16[2,768,128]{2,1,0:T(8,128)(2,1)} %bitcast.149, bf16[2,768,128]{2,1,0:T(8,128)(2,1)} %bitcast.151, bf16[16,2,384,128]{3,2,1,0:T(8,128)(2,1)} %get-tuple-element.77.k_ref, ...), custom_call_target="tpu_custom_call" | custom-call | flops 7549747200 | bytes 14155776 | tf_op jit(solution)/shard_map/pallas_call | solution.py:147
  158.1 46.2 %all-gather.13.cloned.1.call-done = bf16[32,2,384,128]{3,2,1,0:T(8,128)(2,1)} async-done(((bf16[2,2,384,128]{3,2,1,0:T(8,128)(2,1)}), bf16[32,2,384,128]{3,2,1,0:T(8,128)(2,1)}) %all-gather.13.cloned.1.call-update) | async-done | bytes 6291472 | tf_op jit(solution)/shard_map/all_gather | solution.py:198
  204.3 6.3 slice_bitcast_fusion.2
  210.6 8.9 %shard_map.112 = (f32[2,768,128]{2,1,0:T(8,128)}, bf16[16,2,384,128]{3,2,1,0:T(8,128)(2,1)}, bf16[16,2,384,128]{3,2,1,0:T(8,128)(2,1)}) custom-call(s32[3]{0:T(128)} %pad_add_fusion.2.info, bf16[2,768,128]{2,1,0:T(8,128)(2,1)} %bitcast.150, bf16[2,768,128]{2,1,0:T(8,128)(2,1)} %bitcast.152, bf16[16,2,384,128]{3,2,1,0:T(8,128)(2,1)} %get-tuple-element.79.k_ref, ...), custom_call_target="tpu_custom_call" | custom-call | flops 7549747200 | bytes 14155776 | tf_op jit(solution)/shard_map/pallas_call | solution.py:147
  221.1 46.0 %all-gather.15.cloned.1.call-done = bf16[32,2,384,128]{3,2,1,0:T(8,128)(2,1)} async-done(((bf16[2,2,384,128]{3,2,1,0:T(8,128)(2,1)}), bf16[32,2,384,128]{3,2,1,0:T(8,128)(2,1)}) %all-gather.15.cloned.1.call-update) | async-done | bytes 6291472 | tf_op jit(solution)/shard_map/all_gather | solution.py:198
  267.1 6.3 slice_bitcast_fusion
  273.4 8.8 %shard_map.113 = (f32[2,768,128]{2,1,0:T(8,128)}, bf16[16,2,384,128]{3,2,1,0:T(8,128)(2,1)}, bf16[16,2,384,128]{3,2,1,0:T(8,128)(2,1)}) custom-call(s32[3]{0:T(128)} %pad_add_fusion.2.info, bf16[2,768,128]{2,1,0:T(8,128)(2,1)} %bitcast.147, bf16[2,768,128]{2,1,0:T(8,128)(2,1)} %bitcast.148, bf16[16,2,384,128]{3,2,1,0:T(8,128)(2,1)} %get-tuple-element.81.k_ref, ...), custom_call_target="tpu_custom_call" | custom-call | flops 7549747200 | bytes 14155776 | tf_op jit(solution)/shard_map/pallas_call | solution.py:147
  287.0 3.8 multiply_add_fusion.1
  290.8 3.4 fusion.3
  298.8 5.7 fusion.7
  304.5 31.3 %reduce-scatter.9.cloned.1.call-done = bf16[1,2,384,128]{3,2,1,0:T(8,128)(2,1)} async-done(((bf16[16,2,384,128]{3,2,1,0:T(8,128)(2,1)}), bf16[1,2,384,128]{3,2,1,0:T(8,128)(2,1)}) %reduce-scatter.9.cloned.1.call-update) | async-done | bytes 196624 | tf_op jit(solution)/shard_map/reduce_scatter | solution.py:238
  335.8 68.9 %reduce-scatter.11.cloned.1.call-done = bf16[1,2,384,128]{3,2,1,0:T(8,128)(2,1)} async-done(((bf16[16,2,384,128]{3,2,1,0:T(8,128)(2,1)}), bf16[1,2,384,128]{3,2,1,0:T(8,128)(2,1)}) %reduce-scatter.11.cloned.1.call-update) | async-done | bytes 196624 | tf_op jit(solution)/shard_map/reduce_scatter | solution.py:238
  404.7 69.1 %reduce-scatter.13.cloned.1.call-done = bf16[1,2,384,128]{3,2,1,0:T(8,128)(2,1)} async-done(((bf16[16,2,384,128]{3,2,1,0:T(8,128)(2,1)}), bf16[1,2,384,128]{3,2,1,0:T(8,128)(2,1)}) %reduce-scatter.13.cloned.1.call-update) | async-done | bytes 196624 | tf_op jit(solution)/shard_map/reduce_scatter | solution.py:238
  473.8 69.1 %reduce-scatter.15.cloned.1.call-done = bf16[1,2,384,128]{3,2,1,0:T(8,128)(2,1)} async-done(((bf16[16,2,384,128]{3,2,1,0:T(8,128)(2,1)}), bf16[1,2,384,128]{3,2,1,0:T(8,128)(2,1)}) %reduce-scatter.15.cloned.1.call-update) | async-done | bytes 196624 | tf_op jit(solution)/shard_map/reduce_scatter | solution.py:238
  546.9 40.6 %psum.7 = f32[2,128]{1,0:T(2,128)S(1)} all-reduce(f32[2,128]{1,0:T(2,128)S(1)} %pad_maximum_fusion.7), channel_id=1, replica_groups=mesh['ctx'=16,'tp'=2] {'ctx','tp'}, use_global_device_ids=true, to_apply=%region_15.16 | all-reduce | flops 256 | bytes 2048 | tf_op jit(solution)/shard_map/psum | solution.py:249
  588.1 24.6 %reduce-scatter.17.cloned.1.call-done = bf16[1,2,384,128]{3,2,1,0:T(8,128)(2,1)} async-done(((bf16[16,2,384,128]{3,2,1,0:T(8,128)(2,1)}), bf16[1,2,384,128]{3,2,1,0:T(8,128)(2,1)}) %reduce-scatter.17.cloned.1.call-update) | async-done | bytes 196624 | tf_op jit(solution)/shard_map/reduce_scatter | solution.py:239
  612.7 69.0 %reduce-scatter.19.cloned.1.call-done = bf16[1,2,384,128]{3,2,1,0:T(8,128)(2,1)} async-done(((bf16[16,2,384,128]{3,2,1,0:T(8,128)(2,1)}), bf16[1,2,384,128]{3,2,1,0:T(8,128)(2,1)}) %reduce-scatter.19.cloned.1.call-update) | async-done | bytes 196624 | tf_op jit(solution)/shard_map/reduce_scatter | solution.py:239
  681.6 69.1 %reduce-scatter.21.cloned.1.call-done = bf16[1,2,384,128]{3,2,1,0:T(8,128)(2,1)} async-done(((bf16[16,2,384,128]{3,2,1,0:T(8,128)(2,1)}), bf16[1,2,384,128]{3,2,1,0:T(8,128)(2,1)}) %reduce-scatter.21.cloned.1.call-update) | async-done | bytes 196624 | tf_op jit(solution)/shard_map/reduce_scatter | solution.py:239
  750.8 69.0 %reduce-scatter.23.cloned.1.call-done = bf16[1,2,384,128]{3,2,1,0:T(8,128)(2,1)} async-done(((bf16[16,2,384,128]{3,2,1,0:T(8,128)(2,1)}), bf16[1,2,384,128]{3,2,1,0:T(8,128)(2,1)}) %reduce-scatter.23.cloned.1.call-update) | async-done | bytes 196624 | tf_op jit(solution)/shard_map/reduce_scatter | solution.py:239
  (119 shorter events, 44.5 us)
Async XLA Ops:
  7.2 4.4 copy-start.3
  7.2 4.4 copy-start.18
  7.2 71.1 %all-gather.9.cloned.1.call-start = ((), (), s32[]{:S(2)}) async-start(), calls=%async_computation.16 | async-start | bytes 6684672 | tf_op jit(solution)/shard_map/all_gather | solution.py:198
  12.7 4.0 copy-start.16
  12.7 8.3 copy-start.1
  14.0 8.1 copy-start.17
  14.0 127.3 %all-gather.11.cloned.1.call-start = ((), (), s32[]{:S(2)}) async-start(), calls=%async_computation.17 | async-start | bytes 6684672 | tf_op jit(solution)/shard_map/all_gather | solution.py:198
  14.9 189.4 %all-gather.13.cloned.1.call-start = ((), (), s32[]{:S(2)}) async-start(), calls=%async_computation.18 | async-start | bytes 6684672 | tf_op jit(solution)/shard_map/all_gather | solution.py:198
  15.7 251.4 %all-gather.15.cloned.1.call-start = ((), (), s32[]{:S(2)}) async-start(), calls=%async_computation.19 | async-start | bytes 6684672 | tf_op jit(solution)/shard_map/all_gather | solution.py:198
  16.6 319.2 %reduce-scatter.9.cloned.1.call-start = ((), (), s32[]{:S(2)}) async-start(), calls=%async_computation.8 | async-start | bytes 3342336 | tf_op jit(solution)/shard_map/reduce_scatter | solution.py:238
  22.0 2.4 copy-start.13
  24.4 3.8 copy-start.8
  93.5 311.3 %reduce-scatter.11.cloned.1.call-start = ((), (), s32[]{:S(2)}) async-start(), calls=%async_computation.9 | async-start | bytes 3342336 | tf_op jit(solution)/shard_map/reduce_scatter | solution.py:238
  156.4 317.4 %reduce-scatter.13.cloned.1.call-start = ((), (), s32[]{:S(2)}) async-start(), calls=%async_computation.10 | async-start | bytes 3342336 | tf_op jit(solution)/shard_map/reduce_scatter | solution.py:238
  219.5 323.5 %reduce-scatter.15.cloned.1.call-start = ((), (), s32[]{:S(2)}) async-start(), calls=%async_computation.11 | async-start | bytes 3342336 | tf_op jit(solution)/shard_map/reduce_scatter | solution.py:238
  282.3 330.4 %reduce-scatter.17.cloned.1.call-start = ((), (), s32[]{:S(2)}) async-start(), calls=%async_computation.12 | async-start | bytes 3342336 | tf_op jit(solution)/shard_map/reduce_scatter | solution.py:239
  283.0 398.6 %reduce-scatter.19.cloned.1.call-start = ((), (), s32[]{:S(2)}) async-start(), calls=%async_computation.13 | async-start | bytes 3342336 | tf_op jit(solution)/shard_map/reduce_scatter | solution.py:239
  283.6 467.2 %reduce-scatter.21.cloned.1.call-start = ((), (), s32[]{:S(2)}) async-start(), calls=%async_computation.14 | async-start | bytes 3342336 | tf_op jit(solution)/shard_map/reduce_scatter | solution.py:239
  284.3 535.4 %reduce-scatter.23.cloned.1.call-start = ((), (), s32[]{:S(2)}) async-start(), calls=%async_computation.15 | async-start | bytes 3342336 | tf_op jit(solution)/shard_map/reduce_scatter | solution.py:239
  286.9 3.9 copy-start.2
  286.9 3.9 copy-start.7
  290.8 3.5 copy-start
  545.4 277.1 %copy-start.15 = (f32[8,384]{1,0:T(8,128)S(1)}, f32[8,384]{1,0:T(8,128)}, u32[]{:S(2)}) copy-start(f32[8,384]{1,0:T(8,128)} %copy-done.14) | copy-start | bytes 36868
  819.7 2.8 copy-start.5
  (9 other events, 13.3 us)
Sparse Core Ops, SparseCore 0:
  14.1 64.1 all-gather.8
  81.1 60.0 all-gather.10
  144.1 60.0 all-gather.12
  207.0 60.0 all-gather.14
  270.8 64.9 reduce-scatter.8
  339.5 65.2 reduce-scatter.10
  408.5 65.2 reduce-scatter.12
  477.6 65.2 reduce-scatter.14
  546.8 65.8 reduce-scatter.16
  616.3 65.2 reduce-scatter.18
  685.4 65.2 reduce-scatter.20
  754.4 65.2 reduce-scatter.22

commit v2 on v1

--- a/solution.py
+++ b/solution.py
@@ -135,6 +135,175 @@
     dq_ref[0] = dq_acc[...].T * factor
 
 
+def heads_kernel(
+    factor,
+    q_tile,
+    k_tile,
+    width,
+    info,
+    got_ref,
+    begin_ref,
+    out_ref,
+    q_all,
+    up_all,
+    k_all,
+    v_all,
+    dq_all,
+    dk_all,
+    dv_all,
+    held_p,
+    held_dp,
+    held_peak,
+    peak_ref,
+    total_ref,
+    delta_ref,
+    dq_acc,
+):
+    blocks, _, _, rows, head_size = got_ref.shape
+    parts = [pl.ds(at, width) for at in range(0, q_tile, width)]
+
+    @pl.loop(0, blocks)
+    def _(block):
+        span = pl.ds(pl.multiple_of(block * rows, rows), rows)
+        for which, whole in enumerate((q_all, up_all, k_all, v_all)):
+            whole[span, :] = got_ref[block, 0, which]
+        dk_all[span, :] = jnp.zeros((rows, head_size), jnp.float32)
+        dv_all[span, :] = jnp.zeros((rows, head_size), jnp.float32)
+
+    @pl.loop(0, blocks * rows // q_tile)
+    def _(tile):
+        first, clear = info[0, tile], info[1, tile]
+        start = pl.multiple_of(tile * q_tile, q_tile)
+        final = (start + q_tile - 1) // k_tile
+        full = start // k_tile
+        peak_ref[...] = jnp.full(peak_ref.shape, HIDDEN, jnp.float32)
+        total_ref[...] = jnp.zeros(total_ref.shape, jnp.float32)
+        delta_ref[...] = jnp.zeros(delta_ref.shape, jnp.float32)
+        dq_acc[...] = jnp.zeros(dq_acc.shape, jnp.float32)
+
+        def queries(part):
+            return pl.ds(pl.multiple_of(start + part.start, width), width)
+
+        def forward(block, masked):
+            slot = block - first
+            span = pl.ds(pl.multiple_of(block * k_tile, k_tile), k_tile)
+            key_blk = k_all[span, :]
+            value_blk = v_all[span, :]
+            for part in parts:
+                scores = dot(key_blk, q_all[queries(part), :], ((1,), (1,))) * (factor * LOG2E)
+                attend_grad = dot(value_blk, up_all[queries(part), :], ((1,), (1,)))
+                if masked:
+                    key_at = block * k_tile + lax.broadcasted_iota(jnp.int32, scores.shape, 0)
+                    place = start + part.start + lax.broadcasted_iota(jnp.int32, scores.shape, 1)
+                    seen = (key_at >= begin_ref[tile, :, part]) & (key_at <= place)
+                    scores = jnp.where(seen, scores, HIDDEN)
+                old_peak = peak_ref[:, part]
+                peak = jnp.maximum(old_peak, jnp.max(scores, axis=0, keepdims=True))
+                grown = jnp.exp2(scores - peak)
+                shrink = jnp.exp2(old_peak - peak)
+                total_ref[:, part] = total_ref[:, part] * shrink + jnp.sum(
+                    grown, axis=0, keepdims=True
+                )
+                delta_ref[:, part] = delta_ref[:, part] * shrink + jnp.sum(
+                    grown * attend_grad, axis=0, keepdims=True
+                )
+                peak_ref[:, part] = peak
+                held_peak[slot, :, part] = peak
+                held_p[slot, :, part] = grown
+                held_dp[slot, :, part] = attend_grad
+
+        @pl.loop(first, final + 1)
+        def _(block):
+            inside = (block >= clear) & (block < full)
+
+            @pl.when(inside)
+            def _():
+                forward(block, False)
+
+            @pl.when(jnp.logical_not(inside))
+            def _():
+                forward(block, True)
+
+        total_ref[...] = 1.0 / total_ref[...]
+        delta_ref[...] = delta_ref[...] * total_ref[...]
+
+        @pl.loop(first, final + 1)
+        def _(block):
+            slot = block - first
+            span = pl.ds(pl.multiple_of(block * k_tile, k_tile), k_tile)
+            turned_key = k_all[span, :].T
+            dk = dk_all[span, :]
+            dv = dv_all[span, :]
+            for part in parts:
+                weight = jnp.exp2(held_peak[slot, :, part] - peak_ref[:, part]) * total_ref[:, part]
+                attend = held_p[slot, :, part] * weight
+                score_grad = (attend * (held_dp[slot, :, part] - delta_ref[:, part])).astype(
+                    jnp.bfloat16
+                )
+                dv = dv + dot(attend.astype(jnp.bfloat16), up_all[queries(part), :], ((1,), (0,)))
+                dk = dk + dot(score_grad, q_all[queries(part), :], ((1,), (0,)))
+                dq_acc[:, part] += dot(turned_key, score_grad, ((1,), (0,)))
+            dk_all[span, :] = dk
+            dv_all[span, :] = dv
+
+        dq_all[pl.ds(start, q_tile), :] = dq_acc[...].T
+
+    @pl.loop(0, blocks)
+    def _(block):
+        span = pl.ds(pl.multiple_of(block * rows, rows), rows)
+        out_ref[block, 0, 0] = (dq_all[span, :] * factor).astype(out_ref.dtype)
+        out_ref[block, 0, 1] = (dk_all[span, :] * factor).astype(out_ref.dtype)
+        out_ref[block, 0, 2] = dv_all[span, :].astype(out_ref.dtype)
+
+
+def heads_grads(got, documents, reach, factor):
+    blocks, heads, _, rows, head_size = got.shape
+    tokens = blocks * rows
+    q_tile = 512 if tokens % 512 == 0 else rows
+    k_tile = 256 if tokens % 256 == 0 else rows
+    width = 256 if q_tile % 256 == 0 else q_tile
+    slots = min((reach * rows + q_tile - 2) // k_tile + 2, tokens // k_tile)
+    inner = math.gcd(tokens, 128)
+    at = jnp.arange(tokens, dtype=jnp.int32)
+    earlier = jnp.concatenate([documents[:1], documents[:-1]])
+    opened = jnp.where(documents != earlier, at, 0).reshape(-1, inner)
+    lane = jnp.arange(inner)
+    group = jnp.arange(tokens // inner)
+    within = jnp.max(jnp.where(lane[None, :] <= lane[:, None], opened[:, None, :], 0), axis=-1)
+    tops = jnp.max(opened, axis=1)
+    before = jnp.max(jnp.where(group[None, :] < group[:, None], tops[None, :], 0), axis=-1)
+    begin = jnp.maximum(within, before[:, None]).reshape(-1, q_tile)
+    starts = jnp.arange(tokens // q_tile, dtype=jnp.int32) * q_tile
+    lowest = jnp.maximum(begin[:, 0], starts - reach * rows + 1)
+    info = jnp.stack([lowest // k_tile, (begin[:, -1] + k_tile - 1) // k_tile])
+    info = info.astype(jnp.int32)
+    got_spec = pl.BlockSpec((blocks, 1, 4, rows, head_size), lambda g, info: (0, g, 0, 0, 0))
+    out_spec = pl.BlockSpec((blocks, 1, 3, rows, head_size), lambda g, info: (0, g, 0, 0, 0))
+    begin_spec = pl.BlockSpec((tokens // q_tile, 1, q_tile), lambda g, info: (0, 0, 0))
+    whole = pltpu.VMEM((tokens, head_size), jnp.bfloat16)
+    total = pltpu.VMEM((tokens, head_size), jnp.float32)
+    row = pltpu.VMEM((1, q_tile), jnp.float32)
+    return pl.pallas_call(
+        partial(heads_kernel, factor, q_tile, k_tile, width),
+        grid_spec=pltpu.PrefetchScalarGridSpec(
+            num_scalar_prefetch=1,
+            grid=(heads,),
+            in_specs=[got_spec, begin_spec],
+            out_specs=out_spec,
+            scratch_shapes=[whole] * 4
+            + [total] * 3
+            + [pltpu.VMEM((slots, k_tile, q_tile), jnp.float32)] * 2
+            + [pltpu.VMEM((slots, 1, q_tile), jnp.float32)]
+            + [row] * 3
+            + [pltpu.VMEM((head_size, q_tile), jnp.float32)],
+        ),
+        out_shape=jax.ShapeDtypeStruct((blocks, heads, 3, rows, head_size), jnp.bfloat16),
+        compiler_params=pltpu.CompilerParams(
+            dimension_semantics=("arbitrary",), vmem_limit_bytes=60 * 1024 * 1024
+        ),
+    )(info, got, begin[:, None, :])
+
+
 def attend_grads(info, query_rot, upstream, keys, values, begin, place, reach, factor):
     groups, lanes, head_size = query_rot.shape
     blocks, _, rows, _ = keys.shape
@@ -194,12 +363,6 @@
     key_in = jnp.swapaxes(key_raw, 0, 1).astype(jnp.float32)
     key_rot = rotate(key_in, key_gain, cosine, sine_part).astype(jnp.bfloat16)
     value_turned = jnp.swapaxes(values, 0, 1)
-    gathered = [
-        lax.all_gather(
-            jnp.stack([key_rot[at : at + size], value_turned[at : at + size]]), "ctx", axis=0
-        )
-        for at in range(0, groups, size)
-    ]
     query_in = jnp.swapaxes(query_raw, 0, 1).astype(jnp.float32)
     query_rot = (
         rotate(query_in, query_gain, cosine, sine_part)
@@ -208,38 +371,69 @@
     )
     upstream_turned = jnp.swapaxes(upstream, 0, 1).reshape(groups, lanes, head_size)
 
-    own_docs = lax.dynamic_slice_in_dim(documents, first_row, block_rows)
-    begin = jnp.sum((documents[None, :] < own_docs[:, None]).astype(jnp.int32), axis=1)
-    info = jnp.stack(
-        [
-            jnp.maximum(begin[0] // block_rows, own - reach),
-            own,
-            (begin[-1] + block_rows - 1) // block_rows,
+    devices = lax.axis_size("ctx")
+    if query_heads % devices == 0:
+        heads = query_heads // devices
+        sent = jnp.stack(
+            [
+                query_rot.reshape(query_heads, block_rows, head_size),
+                jnp.swapaxes(upstream, 0, 1),
+                jnp.repeat(key_rot, head_grouping, axis=0),
+                jnp.repeat(value_turned, head_grouping, axis=0),
+            ],
+            axis=1,
+        )
+        got = lax.all_to_all(sent, "ctx", 0, 0, tiled=True)
+        made = heads_grads(
+            got.reshape(devices, heads, 4, block_rows, head_size), documents, reach, factor
+        )
+        back = lax.all_to_all(
+            made.reshape(query_heads, 3, block_rows, head_size), "ctx", 0, 0, tiled=True
+        )
+        query_rot_grad = back[:, 0].astype(jnp.float32)
+        shared = back.reshape(groups, head_grouping, 3, block_rows, head_size)
+        key_total = jnp.sum(shared[:, :, 1].astype(jnp.float32), axis=1)
+        value_total = jnp.sum(shared[:, :, 2].astype(jnp.float32), axis=1).astype(jnp.bfloat16)
+    else:
+        gathered = [
+            lax.all_gather(
+                jnp.stack([key_rot[at : at + size], value_turned[at : at + size]]), "ctx", axis=0
+            )
+            for at in range(0, groups, size)
         ]
-    ).astype(jnp.int32)
-    begin_row = jnp.tile(begin, head_grouping)[None, :]
-    place_row = jnp.tile(positions, head_grouping)[None, :]
-
-    dq, dk, dv = [], [], []
-    for index in range(chunks):
-        at = index * size
-        dq_part, dk_part, dv_part = attend_grads(
-            info,
-            query_rot[at : at + size],
-            upstream_turned[at : at + size],
-            gathered[index][:, 0],
-            gathered[index][:, 1],
-            begin_row,
-            place_row,
-            reach,
-            factor,
-        )
-        dq.append(dq_part)
-        dk.append(lax.psum_scatter(dk_part, "ctx", scatter_dimension=0))
-        dv.append(lax.psum_scatter(dv_part, "ctx", scatter_dimension=0))
-    query_rot_grad = jnp.concatenate(dq).reshape(query_heads, block_rows, head_size)
-    key_total = jnp.concatenate(dk).astype(jnp.float32)
-    value_total = jnp.concatenate(dv)
+        own_docs = lax.dynamic_slice_in_dim(documents, first_row, block_rows)
+        begin = jnp.sum((documents[None, :] < own_docs[:, None]).astype(jnp.int32), axis=1)
+        info = jnp.stack(
+            [
+                jnp.maximum(begin[0] // block_rows, own - reach),
+                own,
+                (begin[-1] + block_rows - 1) // block_rows,
+            ]
+        ).astype(jnp.int32)
+        begin_row = jnp.tile(begin, head_grouping)[None, :]
+        place_row = jnp.tile(positions, head_grouping)[None, :]
+
+        dq, dk, dv = [], [], []
+        for index in range(chunks):
+            at = index * size
+            dq_part, dk_part, dv_part = attend_grads(
+                info,
+                query_rot[at : at + size],
+                upstream_turned[at : at + size],
+                gathered[index][:, 0],
+                gathered[index][:, 1],
+                begin_row,
+                place_row,
+                reach,
+                factor,
+            )
+            dq.append(dq_part)
+            dk.append(lax.psum_scatter(dk_part, "ctx", scatter_dimension=0))
+            dv.append(lax.psum_scatter(dv_part, "ctx", scatter_dimension=0))
+        query_rot_grad = jnp.concatenate(dq).reshape(query_heads, block_rows, head_size)
+        key_total = jnp.concatenate(dk).astype(jnp.float32)
+        value_total = jnp.concatenate(dv)
+
 
     turn = lambda inputs, gain_vec: rotate(inputs, gain_vec, cosine, sine_part)
     _, query_pull = jax.vjp(turn, query_in, query_gain)

time: 833 us -> 388 us (0.47)
  waiting for transfers between devices: 659 us -> 110 us
  blocking collectives: 40.6 us -> 172 us
  local copies, waits for them, and re-layouts: 44.3 us -> 9.17 us
  Pallas kernels: 35.4 us -> 58.7 us
  between operations: 17.2 us -> 1.05 us
    reduce_scatter x8 -> x0, waiting for transfers between devices: 470 us -> none  [the longest x4 238 us: on_device(): dk.append(lax.psum_scatter(dk_part, 'ctx', scatter_dimension=0))]
    all_gather x4 -> x0, waiting for transfers between devices: 186 us -> none  [on_device(): lax.all_gather(jnp.stack([key_rot[at:at + size], value_turned[at:at + siz...]
    all_to_all x0 -> x1, blocking collectives: none -> 131 us  [on_device(): lax.all_to_all(made.reshape(query_heads, 3, block_rows, head_size), 'ctx'...]
    all_to_all x0 -> x1, waiting for transfers between devices: none -> 110 us  [on_device(): got = lax.all_to_all(sent, 'ctx', 0, 0, tiled=True)]
    squeeze x4 -> x0, local copies, waits for them, and re-layouts: 25.1 us -> none  [on_device(): gathered[index][:, 1]]
    pallas_call x4 -> x1, Pallas kernels: 35.4 us -> 58.7 us  [heads_grads(): pl.pallas_call(partial(heads_kernel, factor, q_tile, k_tile, width), grid...]
  transfers between devices with their start and end apart: 12 -> 1, of which waited for: 12 -> 1; matrix products, arithmetic and copies ran while one was open for 8% -> 1% of each run, Pallas kernels for 4% -> 0%
where the time goes in v2:
time: 388 us; the launch traced here: 387 us
  blocking collectives  172 us (44%)
  waiting for transfers between devices  110 us (28%)
  Pallas kernels  58.7 us (15%)
  other arithmetic  29.2 us (8%)
  local copies, waits for them, and re-layouts  9.17 us (2%)
  starting transfers between devices  7.56 us (2%)
    all_to_all x1, blocking collectives, on_device(): lax.all_to_all(made.reshape(query_heads, 3, block_rows, head_size), 'ctx'...  131 us
    all_to_all x1, waiting for transfers between devices, on_device(): got = lax.all_to_all(sent, 'ctx', 0, 0, tiled=True)  110 us
    pallas_call x1, Pallas kernels, heads_grads(): pl.pallas_call(partial(heads_kernel, factor, q_tile, k_tile, width), grid...  58.7 us
    psum x1, blocking collectives, on_device(): lax.psum(jnp.stack([query_gain_part, key_gain_part]), ('ctx', 'tp'))  40.4 us
    unnamed x40, local copies, waits for them, and re-layouts  7.79 us
  transfers between devices with their start and end apart: 1, of which 1 were waited for; matrix products, arithmetic and copies ran while one was open for 1% of the time, Pallas kernels for 0%

profile of v2, /device:TPU:0, one launch (start us, length us, event | category | flops | bytes accessed | tf_op | source)
XLA Modules:
  0.0 387.5 jit_solution(13447528481263016357)
XLA Ops:
  0.7 1.7 fusion.15
  3.0 2.4 fusion.4
  5.4 0.8 multiply_sine_fusion
  6.8 0.7 copy-done.3
  8.0 0.9 copy-done.1
  8.9 0.9 fusion.2
  10.4 1.1 fusion.7
  12.6 3.8 pad_maximum_fusion
  16.3 7.6 %all-to-all-start = ((bf16[16,4,384,128]{3,2,1,0:T(8,128)(2,1)}), bf16[16,4,384,128]{3,2,1,0:T(8,128)(2,1)}, u32[]{:S(2)}, u32[]{:S(2)}) async-start(bf16[16,4,384,128]{3,2,1,0:T(8,128)(2,1)} %pad_maximum_fusion), calls=%async_computation | async-start | bytes 12582912 | tf_op jit(solution)/shard_map/all_to_all | solution.py:386
  24.4 0.8 fusion.21
  25.6 0.9 select_reduce_fusion
  27.9 110.0 %all-to-all-done = bf16[16,4,384,128]{3,2,1,0:T(8,128)(2,1)} async-done(((bf16[16,4,384,128]{3,2,1,0:T(8,128)(2,1)}), bf16[16,4,384,128]{3,2,1,0:T(8,128)(2,1)}, u32[]{:S(2)}, u32[]{:S(2)}) %all-to-all-start) | async-done | bytes 6291488 | tf_op jit(solution)/shard_map/all_to_all | solution.py:386
  138.0 58.7 %shard_map.110 = bf16[16,1,3,384,128]{4,3,2,1,0:T(8,128)(2,1)} custom-call(s32[2,12]{1,0:T(2,128)} %pad_add_fusion.2.info, bf16[16,1,4,384,128]{4,3,2,1,0:T(8,128)(2,1)} %bitcast.11.got_ref, s32[12,1,512]{2,1,0:T(1,128)} %max.40.begin_ref), custom_call_target="tpu_custom_call" | custom-call | tf_op jit(solution)/shard_map/pallas_call | solution.py:286
  196.6 131.4 %all_to_all.10 = bf16[16,3,384,128]{3,2,1,0:T(8,128)(2,1)S(1)} all-to-all(bf16[16,3,384,128]{3,2,1,0:T(8,128)(2,1)} %bitcast.102), channel_id=1, replica_groups=mesh['ctx'=16,'tp'=2] {'ctx'}, dimensions={0} | all-to-all | bytes 9437184 | tf_op jit(solution)/shard_map/all_to_all | solution.py:390
  328.6 1.4 copy.55
  330.0 0.7 multiply_add_fusion.3
  330.7 1.5 fusion.14
  332.2 1.5 fusion.17
  333.7 1.4 copy.54
  335.4 1.2 multiply_add_fusion.1
  336.8 2.8 fusion.3
  339.6 40.4 %psum.7 = f32[2,128]{1,0:T(2,128)S(1)} all-reduce(f32[2,128]{1,0:T(2,128)S(1)} %pad_maximum_fusion.2), channel_id=1, replica_groups=mesh['ctx'=16,'tp'=2] {'ctx','tp'}, use_global_device_ids=true, to_apply=%region_11.12 | all-reduce | flops 256 | bytes 2048 | tf_op jit(solution)/shard_map/psum | solution.py:443
  380.0 4.7 %fusion.9 = bf16[384,16,128]{2,0,1:T(8,128)(2,1)S(1)} fusion(f32[16,384]{1,0:T(8,128)S(1)} %multiply_multiply_fusion, f32[128]{0:T(128)S(1)} %copy-done.14, f32[16,384]{1,0:T(8,128)S(1)} %copy-done.8, bf16[384,16,128]{2,1,0:T(8,128)(2,1)} %param.7, f32[16,384,64]{2,1,0:T(8,128)} %copy-done, f32[16,384,64]{2,1,0:T(8,128)S(1)} %get-tuple-element.42), kind=kLoop, calls=%fused_computation.23 | loop fusion | flops 6291456 | bytes 6341120 | tf_op jit(solution)/shard_map/transpose | solution.py:446
  384.8 2.2 copy.53
  (63 shorter events, 7.2 us)
Async XLA Ops:
  0.6 5.6 %copy-start.5 = (bf16[384,8,128]{2,1,0:T(8,128)(2,1)S(1)}, bf16[384,8,128]{2,1,0:T(8,128)(2,1)}, u32[]{:S(2)}) copy-start(bf16[384,8,128]{2,1,0:T(8,128)(2,1)} %param.9) | copy-start | bytes 2359300
  2.4 0.6 copy-start.11
  3.0 3.3 copy-start.4
  5.4 1.4 copy-start.9
  5.4 2.5 copy-start.6
  6.3 1.1 copy-start.3
  6.3 1.1 copy-start.15
  7.5 1.4 copy-start.1
  7.5 1.4 copy-start.14
  16.3 7.6 %copy-start.13 = (s32[6144]{0:T(1024)S(1)}, s32[6144]{0:T(1024)}, u32[]{:S(2)}) copy-start(s32[6144]{0:T(1024)} %param.12) | copy-start | bytes 73732
  16.3 121.6 %all-to-all-start = ((bf16[16,4,384,128]{3,2,1,0:T(8,128)(2,1)}), bf16[16,4,384,128]{3,2,1,0:T(8,128)(2,1)}, u32[]{:S(2)}, u32[]{:S(2)}) async-start(bf16[16,4,384,128]{3,2,1,0:T(8,128)(2,1)} %pad_maximum_fusion), calls=%async_computation | async-start | bytes 12582912 | tf_op jit(solution)/shard_map/all_to_all | solution.py:386
  330.0 0.7 copy-start.16
  330.7 1.5 copy-start.12
  335.4 1.4 copy-start.2
  335.4 1.4 copy-start.7
  336.6 2.9 copy-start
  336.8 43.2 %copy-start.10 = (f32[16,384]{1,0:T(8,128)S(1)}, f32[16,384]{1,0:T(8,128)}, u32[]{:S(2)}) copy-start(f32[16,384]{1,0:T(8,128)} %copy-done.9) | copy-start | bytes 73732
  336.8 43.2 %copy-start.8 = (f32[16,384]{1,0:T(8,128)S(1)}, f32[16,384]{1,0:T(8,128)}, u32[]{:S(2)}) copy-start(f32[16,384]{1,0:T(8,128)} %copy-done.6) | copy-start | bytes 73732

commit v3 on v2

--- a/solution.py
+++ b/solution.py
@@ -142,8 +142,10 @@
     width,
     info,
     got_ref,
+    other_ref,
     begin_ref,
     out_ref,
+    give_ref,
     q_all,
     up_all,
     k_all,
@@ -165,8 +167,19 @@
     @pl.loop(0, blocks)
     def _(block):
         span = pl.ds(pl.multiple_of(block * rows, rows), rows)
-        for which, whole in enumerate((q_all, up_all, k_all, v_all)):
-            whole[span, :] = got_ref[block, 0, which]
+        q_all[span, :] = got_ref[block, 0, 0]
+        up_all[span, :] = got_ref[block, 0, 1]
+
+        @pl.when(info[2, 0] == 0)
+        def _():
+            k_all[span, :] = got_ref[block, 0, 2]
+            v_all[span, :] = other_ref[block]
+
+        @pl.when(info[2, 0] != 0)
+        def _():
+            k_all[span, :] = other_ref[block]
+            v_all[span, :] = got_ref[block, 0, 2]
+
         dk_all[span, :] = jnp.zeros((rows, head_size), jnp.float32)
         dv_all[span, :] = jnp.zeros((rows, head_size), jnp.float32)
 
@@ -252,11 +265,21 @@
     def _(block):
         span = pl.ds(pl.multiple_of(block * rows, rows), rows)
         out_ref[block, 0, 0] = (dq_all[span, :] * factor).astype(out_ref.dtype)
-        out_ref[block, 0, 1] = (dk_all[span, :] * factor).astype(out_ref.dtype)
-        out_ref[block, 0, 2] = dv_all[span, :].astype(out_ref.dtype)
-
-
-def heads_grads(got, documents, reach, factor):
+        dk = (dk_all[span, :] * factor).astype(out_ref.dtype)
+        dv = dv_all[span, :].astype(out_ref.dtype)
+
+        @pl.when(info[2, 0] == 0)
+        def _():
+            out_ref[block, 0, 1] = dk
+            give_ref[block] = dv
+
+        @pl.when(info[2, 0] != 0)
+        def _():
+            out_ref[block, 0, 1] = dv
+            give_ref[block] = dk
+
+
+def heads_grads(got, other, parity, documents, reach, factor):
     blocks, heads, _, rows, head_size = got.shape
     tokens = blocks * rows
     q_tile = 512 if tokens % 512 == 0 else rows
@@ -275,10 +298,17 @@
     begin = jnp.maximum(within, before[:, None]).reshape(-1, q_tile)
     starts = jnp.arange(tokens // q_tile, dtype=jnp.int32) * q_tile
     lowest = jnp.maximum(begin[:, 0], starts - reach * rows + 1)
-    info = jnp.stack([lowest // k_tile, (begin[:, -1] + k_tile - 1) // k_tile])
+    info = jnp.stack(
+        [
+            lowest // k_tile,
+            (begin[:, -1] + k_tile - 1) // k_tile,
+            jnp.full(starts.shape, parity, jnp.int32),
+        ]
+    )
     info = info.astype(jnp.int32)
-    got_spec = pl.BlockSpec((blocks, 1, 4, rows, head_size), lambda g, info: (0, g, 0, 0, 0))
-    out_spec = pl.BlockSpec((blocks, 1, 3, rows, head_size), lambda g, info: (0, g, 0, 0, 0))
+    got_spec = pl.BlockSpec((blocks, 1, 3, rows, head_size), lambda g, info: (0, g, 0, 0, 0))
+    other_spec = pl.BlockSpec((blocks, rows, head_size), lambda g, info: (0, 0, 0))
+    out_spec = pl.BlockSpec((blocks, 1, 2, rows, head_size), lambda g, info: (0, g, 0, 0, 0))
     begin_spec = pl.BlockSpec((tokens // q_tile, 1, q_tile), lambda g, info: (0, 0, 0))
     whole = pltpu.VMEM((tokens, head_size), jnp.bfloat16)
     total = pltpu.VMEM((tokens, head_size), jnp.float32)
@@ -288,8 +318,8 @@
         grid_spec=pltpu.PrefetchScalarGridSpec(
             num_scalar_prefetch=1,
             grid=(heads,),
-            in_specs=[got_spec, begin_spec],
-            out_specs=out_spec,
+            in_specs=[got_spec, other_spec, begin_spec],
+            out_specs=[out_spec, other_spec],
             scratch_shapes=[whole] * 4
             + [total] * 3
             + [pltpu.VMEM((slots, k_tile, q_tile), jnp.float32)] * 2
@@ -297,11 +327,14 @@
             + [row] * 3
             + [pltpu.VMEM((head_size, q_tile), jnp.float32)],
         ),
-        out_shape=jax.ShapeDtypeStruct((blocks, heads, 3, rows, head_size), jnp.bfloat16),
+        out_shape=(
+            jax.ShapeDtypeStruct((blocks, heads, 2, rows, head_size), jnp.bfloat16),
+            jax.ShapeDtypeStruct(other.shape, jnp.bfloat16),
+        ),
         compiler_params=pltpu.CompilerParams(
             dimension_semantics=("arbitrary",), vmem_limit_bytes=60 * 1024 * 1024
         ),
-    )(info, got, begin[:, None, :])
+    )(info, got, other, begin[:, None, :])
 
 
 def attend_grads(info, query_rot, upstream, keys, values, begin, place, reach, factor):
@@ -372,28 +405,29 @@
     upstream_turned = jnp.swapaxes(upstream, 0, 1).reshape(groups, lanes, head_size)
 
     devices = lax.axis_size("ctx")
-    if query_heads % devices == 0:
-        heads = query_heads // devices
+    if query_heads == devices and head_grouping == 2:
+        swap = [(index, index ^ 1) for index in range(devices)]
+        halves = jnp.stack([key_rot, value_turned], axis=1)
         sent = jnp.stack(
             [
                 query_rot.reshape(query_heads, block_rows, head_size),
                 jnp.swapaxes(upstream, 0, 1),
-                jnp.repeat(key_rot, head_grouping, axis=0),
-                jnp.repeat(value_turned, head_grouping, axis=0),
+                halves.reshape(query_heads, block_rows, head_size),
             ],
             axis=1,
         )
         got = lax.all_to_all(sent, "ctx", 0, 0, tiled=True)
-        made = heads_grads(
-            got.reshape(devices, heads, 4, block_rows, head_size), documents, reach, factor
-        )
+        other = lax.ppermute(got[:, 2], "ctx", swap)
+        made, give = heads_grads(got[:, None], other, own % 2, documents, reach, factor)
+        taken = lax.ppermute(give, "ctx", swap)
+        summed = (made[:, 0, 1].astype(jnp.float32) + taken.astype(jnp.float32)).astype(jnp.bfloat16)
         back = lax.all_to_all(
-            made.reshape(query_heads, 3, block_rows, head_size), "ctx", 0, 0, tiled=True
+            jnp.stack([made[:, 0, 0], summed], axis=1), "ctx", 0, 0, tiled=True
         )
         query_rot_grad = back[:, 0].astype(jnp.float32)
-        shared = back.reshape(groups, head_grouping, 3, block_rows, head_size)
-        key_total = jnp.sum(shared[:, :, 1].astype(jnp.float32), axis=1)
-        value_total = jnp.sum(shared[:, :, 2].astype(jnp.float32), axis=1).astype(jnp.bfloat16)
+        shared = back[:, 1].reshape(groups, 2, block_rows, head_size)
+        key_total = shared[:, 0].astype(jnp.float32)
+        value_total = shared[:, 1]
     else:
         gathered = [
             lax.all_gather(
@@ -440,7 +474,10 @@
     _, key_pull = jax.vjp(turn, key_in, key_gain)
     query_in_grad, query_gain_part = query_pull(query_rot_grad)
     key_in_grad, key_gain_part = key_pull(key_total)
-    gain_sums = lax.psum(jnp.stack([query_gain_part, key_gain_part]), ("ctx", "tp"))
+    parts = jnp.stack([query_gain_part, key_gain_part])
+    everyone = lax.axis_size("ctx") * lax.axis_size("tp")
+    spread = jnp.broadcast_to(parts[None], (everyone,) + parts.shape)
+    gain_sums = jnp.sum(lax.all_to_all(spread, ("ctx", "tp"), 0, 0, tiled=True), axis=0)
     rescale = 1.0 / math.sqrt(lax.axis_size("ctx") * block_rows)
     return (
         jnp.swapaxes(query_in_grad.astype(jnp.bfloat16), 0, 1),

time: 388 us -> 322 us (0.83)
  waiting for transfers between devices: 110 us -> 2.41 us
  local copies, waits for them, and re-layouts: 9.17 us -> 24.7 us
  blocking collectives: 172 us -> 185 us
  Pallas kernels: 58.7 us -> 64.9 us
  other arithmetic: 29.2 us -> 35.4 us
    all_to_all x1, waiting for transfers between devices: 110 us -> 0.51 us  [on_device(): lax.all_to_all(spread, ('ctx', 'tp'), 0, 0, tiled=True)]
    all_to_all x1 -> x2, blocking collectives: 131 us -> 185 us  [the longest x1 111 us: on_device(): got = lax.all_to_all(sent, 'ctx', 0, 0, tiled=True)]
    psum x1 -> x0, blocking collectives: 40.4 us -> none  [on_device(): lax.psum(jnp.stack([query_gain_part, key_gain_part]), ('ctx', 'tp'))]
    pallas_call x1, Pallas kernels: 58.7 us -> 64.9 us  [heads_grads(): pl.pallas_call(partial(heads_kernel, factor, q_tile, k_tile, width), grid...]
    unnamed x40 -> x63, local copies, waits for them, and re-layouts: 7.79 us -> 12 us
  transfers between devices with their start and end apart: 1 -> 3, of which waited for: 1 -> 2; matrix products, arithmetic and copies ran while one was open for 1% -> 7% of each run, Pallas kernels for 0% -> 0%
where the time goes in v3:
time: 322 us; the launch traced here: 320 us
  blocking collectives  185 us (57%)
  Pallas kernels  64.9 us (20%)
  other arithmetic  35.4 us (11%)
  local copies, waits for them, and re-layouts  24.7 us (8%)
  starting transfers between devices  6.34 us (2%)
    all_to_all x1, blocking collectives, on_device(): got = lax.all_to_all(sent, 'ctx', 0, 0, tiled=True)  111 us
    all_to_all x1, blocking collectives, on_device(): lax.all_to_all(jnp.stack([made[:, 0, 0], summed], axis=1), 'ctx', 0, 0, t...  74.2 us
    pallas_call x1, Pallas kernels, heads_grads(): pl.pallas_call(partial(heads_kernel, factor, q_tile, k_tile, width), grid...  64.9 us
    unnamed x63, local copies, waits for them, and re-layouts  12 us
  transfers between devices with their start and end apart: 3, of which 2 were waited for; matrix products, arithmetic and copies ran while one was open for 7% of the time, Pallas kernels for 0%

profile of v3, /device:TPU:0, one launch (start us, length us, event | category | flops | bytes accessed | tf_op | source)
XLA Modules:
  0.0 319.6 jit_solution(1649888666654039482)
XLA Ops:
  0.7 2.4 fusion.5
  13.4 110.5 %all_to_all.15 = bf16[16,3,384,128]{3,2,1,0:T(8,128)(2,1)S(1)} all-to-all(bf16[16,3,384,128]{3,2,1,0:T(8,128)(2,1)S(1)} %pad_maximum_fusion), channel_id=1, replica_groups=mesh['ctx'=16,'tp'=2] {'ctx'}, dimensions={0} | all-to-all | bytes 9437184 | tf_op jit(solution)/shard_map/all_to_all | solution.py:419
  123.9 2.1 copy-done
  129.0 2.2 fusion.25
  131.9 1.3 max.34
  135.2 2.2 select_reduce_fusion
  137.4 1.4 reduce_max.32
  138.8 1.4 max.40.begin_ref
  141.2 1.3 add_add_fusion.2.info
  143.6 64.9 %shard_map.110 = (bf16[16,1,2,384,128]{4,3,2,1,0:T(8,128)(2,1)}, bf16[16,384,128]{2,1,0:T(8,128)(2,1)}) custom-call(s32[3,12]{1,0:T(4,128)} %add_add_fusion.2.info, bf16[16,1,3,384,128]{4,3,2,1,0:T(8,128)(2,1)} %bitcast.121, bf16[16,384,128]{2,1,0:T(8,128)(2,1)} %copy-done.16, s32[12,1,512]{2,1,0:T(1,128)} %max.40.begin_ref), custom_call_target="tpu_custom_call" | custom-call | tf_op jit(solution)/shard_map/pallas_call | solution.py:316
  208.5 1.7 slice_bitcast_fusion.2
  210.2 1.9 collective-permute-done.1
  213.1 74.2 %all_to_all.16 = bf16[16,2,384,128]{3,2,1,0:T(8,128)(2,1)S(1)} all-to-all(bf16[16,2,384,128]{3,2,1,0:T(8,128)(2,1)S(1)} %copy.101), channel_id=1, replica_groups=mesh['ctx'=16,'tp'=2] {'ctx'}, dimensions={0} | all-to-all | bytes 6291456 | tf_op jit(solution)/shard_map/all_to_all | solution.py:424
  290.4 2.3 fusion.15
  292.7 1.6 copy.104
  294.3 1.3 multiply_multiply_fusion.1
  295.6 1.5 copy.105
  297.1 1.3 multiply_add_fusion.1
  298.5 2.7 fusion.4
  301.4 3.6 %fusion.11 = bf16[384,16,128]{2,0,1:T(8,128)(2,1)} fusion(f32[16,384]{1,0:T(8,128)S(1)} %multiply_multiply_fusion, f32[128]{0:T(128)S(1)} %copy-done.24, f32[16,384]{1,0:T(8,128)S(1)} %copy-done.20, bf16[384,16,128]{2,1,0:T(8,128)(2,1)S(1)} %copy-done.2, f32[16,384,64]{2,1,0:T(8,128)S(1)} %get-tuple-element.62, f32[16,384,64]{2,1,0:T(8,128)S(1)} %get-tuple-element.61), kind=kLoop, calls=%fused_computation.26 | loop fusion | flops 6291456 | bytes 6341120 | tf_op jit(solution)/shard_map/transpose | solution.py:483
  305.6 5.3 %all-to-all-start.2 = ((f32[32,2,128]{2,1,0:T(2,128)}), f32[32,2,128]{2,1,0:T(2,128)}, u32[]{:S(2)}, u32[]{:S(2)}) async-start(f32[32,2,128]{2,1,0:T(2,128)} %broadcast_in_dim.52), calls=%async_computation.2 | async-start | bytes 65536 | tf_op jit(solution)/shard_map/all_to_all | solution.py:480
  311.0 3.2 fusion.20
  314.2 1.4 copy.132
  315.6 2.2 copy.108
  (100 shorter events, 24.5 us)
Async XLA Ops:
  0.6 3.0 copy-start.7
  0.7 4.5 %copy-start.25 = (f32[128]{0:T(128)S(1)}, f32[128]{0:T(128)}, u32[]{:S(2)}) copy-start(f32[128]{0:T(128)} %param.11) | copy-start | bytes 1540
  3.7 5.4 %copy-start.19 = (f32[16,384]{1,0:T(8,128)}, f32[16,384]{1,0:T(8,128)S(1)}, u32[]{:S(2)}) copy-start(f32[16,384]{1,0:T(8,128)S(1)} %fusion.22) | copy-start | bytes 73732
  4.4 2.0 copy-start.12
  7.3 1.4 copy-start.15
  8.7 1.4 copy-start.1
  8.7 1.4 copy-start.24
  123.9 2.1 copy-start
  126.2 16.3 %collective-permute-start = (bf16[16,384,128]{2,1,0:T(8,128)(2,1)S(1)}, bf16[16,384,128]{2,1,0:T(8,128)(2,1)S(1)}, u32[]{:S(2)}, u32[]{:S(2)}) collective-permute-start(bf16[16,384,128]{2,1,0:T(8,128)(2,1)S(1)} %slice_bitcast_fusion.3), channel_id=1, source_target_pairs={{0,2},{2,0},{4,6},{6,4},{8,10},{10,8},{12,14},{14,12},{16,18},{18,... | collective-permute-start | bytes 4718600 | tf_op jit(solution)/shard_map/ppermute | solution.py:420
  208.5 3.6 %collective-permute-start.1 = (bf16[16,384,128]{2,1,0:T(8,128)(2,1)}, bf16[16,384,128]{2,1,0:T(8,128)(2,1)S(1)}, u32[]{:S(2)}, u32[]{:S(2)}) collective-permute-start(bf16[16,384,128]{2,1,0:T(8,128)(2,1)} %get-tuple-element.12), channel_id=1, source_target_pairs={{0,2},{2,0},{4,6},{6,4},{8,10},{10,8},{12,14},{14,12},{16,18},{18,... | collective-permute-start | bytes 4718600 | tf_op jit(solution)/shard_map/ppermute | solution.py:422
  208.5 3.6 %copy-start.10 = (bf16[16,1,2,384,128]{4,3,2,1,0:T(8,128)(2,1)S(1)}, bf16[16,1,2,384,128]{4,3,2,1,0:T(8,128)(2,1)}, u32[]{:S(2)}) copy-start(bf16[16,1,2,384,128]{4,3,2,1,0:T(8,128)(2,1)} %get-tuple-element.11) | copy-start | bytes 9437188
  290.1 2.6 copy-start.3
  290.1 2.6 copy-start.5
  297.1 1.4 copy-start.2
  297.1 1.4 copy-start.20
  298.5 2.7 copy-start.23
  301.3 3.7 %copy-start.28 = (f32[128]{0:T(128)S(1)}, f32[128]{0:T(128)}, u32[]{:S(2)}) copy-start(f32[128]{0:T(128)} %get-tuple-element.55) | copy-start | bytes 1540
  301.3 9.6 %copy-start.4 = (f32[8,384,64]{2,0,1:T(8,128)S(1)}, f32[8,384,64]{2,0,1:T(8,128)}, u32[]{:S(2)}) copy-start(f32[8,384,64]{2,0,1:T(8,128)} %copy-done.3) | copy-start | bytes 2359300
  301.3 9.6 %copy-start.6 = (f32[8,384,64]{2,0,1:T(8,128)S(1)}, f32[8,384,64]{2,0,1:T(8,128)}, u32[]{:S(2)}) copy-start(f32[8,384,64]{2,0,1:T(8,128)} %copy-done.5) | copy-start | bytes 2359300
  301.3 9.6 %copy-start.14 = (f32[8,384]{0,1:T(8,128)S(1)}, f32[8,384]{0,1:T(8,128)}, u32[]{:S(2)}) copy-start(f32[8,384]{0,1:T(8,128)} %copy-done.12) | copy-start | bytes 36868
  301.3 9.6 %copy-start.18 = (f32[8,384]{0,1:T(8,128)S(1)}, f32[8,384]{0,1:T(8,128)}, u32[]{:S(2)}) copy-start(f32[8,384]{0,1:T(8,128)} %copy.105) | copy-start | bytes 36868
  301.4 9.6 %copy-start.27 = (f32[128]{0:T(128)S(1)}, f32[128]{0:T(128)}, u32[]{:S(2)}) copy-start(f32[128]{0:T(128)} %param.11) | copy-start | bytes 1540
  305.6 12.6 %all-to-all-start.2 = ((f32[32,2,128]{2,1,0:T(2,128)}), f32[32,2,128]{2,1,0:T(2,128)}, u32[]{:S(2)}, u32[]{:S(2)}) async-start(f32[32,2,128]{2,1,0:T(2,128)} %broadcast_in_dim.52), calls=%async_computation.2 | async-start | bytes 65536 | tf_op jit(solution)/shard_map/all_to_all | solution.py:480
  311.0 3.2 %copy-start.11 = (bf16[8,1,384,128]{3,2,1,0:T(8,128)(2,1)S(1)}, bf16[8,1,384,128]{3,2,1,0:T(8,128)(2,1)}, u32[]{:S(2)}) copy-start(bf16[8,1,384,128]{3,2,1,0:T(8,128)(2,1)} %get-tuple-element.71) | copy-start | bytes 2359300
  (8 other events, 8.3 us)
